TPU v7x, 512 devices: a whole 4x4x16 slice. The times are simulated.
512 devices in a mesh: dp: 4 (over y), grp: 4 (over x), loc: 32 (over z, core).
Axes of the slice: x: 4, y: 4, z: 16, core: 2. Of those that a mesh axis runs over, the one named last changes fastest.
Arguments:
- tokens: bfloat16 [16384, 2048], P(('grp', 'loc'), 'dp'), may hold values from -6 to 6
- grad_out: bfloat16 [16384, 2048], P(('grp', 'loc'), 'dp'), may hold values from -6 to 6
- expert_ids: int32 [16384, 4], P(('grp', 'loc')), may hold values from 0 to 127, all different within a row; in each aligned block of 128 rows (0 to 127, 128 to 255, ...) at most 8 rows name the same one
- gate_scale: float32 [16384, 4], P(('grp', 'loc')), may hold values from 0.1 to 1
- gate_weight: bfloat16 [128, 768, 2048], P(('grp', 'loc'), 'dp'), may hold values from -0.125 to 0.125
- up_weight: bfloat16 [128, 768, 2048], P(('grp', 'loc'), 'dp'), may hold values from -0.125 to 0.125
- down_weight: bfloat16 [128, 768, 2048], P(('grp', 'loc'), None, 'dp'), may hold values from -0.21875 to 0.21875
Outputs:
- layer_out: bfloat16 [16384, 2048], P(('grp', 'loc'), 'dp')
- gate_gradient: bfloat16 [128, 768, 2048], P(('grp', 'loc'), 'dp')
- up_gradient: bfloat16 [128, 768, 2048], P(('grp', 'loc'), 'dp')
- down_gradient: bfloat16 [128, 768, 2048], P(('grp', 'loc'), None, 'dp')
Inputs may be any that keep to these rules, and one draw needn't show every extreme that they name: `expert_ids`: each token names 4 different experts. Within one index of grp and loc (aligned blocks of 128 token rows) no expert is named by more than 8 rows, a bound that some block reaches.
All inputs are finite; a program needn't handle non-finite values.
Results may differ from a plain program's by a relative error of at most 0.0058.
Values may be sent and summed in bfloat16 or wider, within the bound.
A program may use at most 64 MiB of HBM per device.

v0:
```python
import jax
import jax.numpy as jnp
from jax import lax
from jax.sharding import PartitionSpec as P


def slot_layout(route_ids, experts, capacity):
    flat_ids = route_ids.reshape(-1)
    onehot = (
        flat_ids[:, None] == lax.broadcasted_iota(jnp.int32, (flat_ids.shape[0], experts), 1)
    ).astype(jnp.int32)
    ranks = jnp.sum((jnp.cumsum(onehot, axis=0) - 1) * onehot, axis=1)
    return flat_ids * capacity + ranks


def place_matrix(positions, tok_rows, per_token, slots_total):
    slot_index = lax.broadcasted_iota(jnp.int32, (slots_total, tok_rows, per_token), 0)
    hits = slot_index == positions.reshape(1, tok_rows, per_token)
    return jnp.sum(hits.astype(jnp.float32), axis=2).astype(jnp.bfloat16)


def send_rows(outgoing):
    return lax.all_to_all(outgoing, ("grp", "loc"), split_axis=0, concat_axis=0, tiled=True)


def return_rows(results):
    return lax.all_to_all(results, ("grp", "loc"), split_axis=0, concat_axis=0, tiled=True)


def body(tokens, grad_out, expert_ids, gate_scale, gate_weight, up_weight, down_weight):
    tok_rows, quarter = tokens.shape
    per_token = expert_ids.shape[1]
    experts = lax.axis_size(("grp", "loc"))
    capacity = min(tok_rows, max(2, 2 * tok_rows * per_token // experts))
    slots_total = experts * capacity
    positions = slot_layout(expert_ids, experts, capacity)
    unit_place = place_matrix(positions, tok_rows, per_token, slots_total)
    slot_scale = jnp.zeros((slots_total,), jnp.float32).at[positions].set(gate_scale.reshape(-1))
    picked_grads = jnp.dot(unit_place, grad_out, preferred_element_type=jnp.float32)
    grad_rows = (picked_grads * slot_scale[:, None]).astype(jnp.bfloat16)
    full_tokens = lax.all_gather(tokens, "dp", axis=1, tiled=True)
    features = full_tokens.shape[1]
    token_rows = jnp.dot(unit_place, full_tokens, preferred_element_type=jnp.float32).astype(
        jnp.bfloat16
    )
    outgoing = jnp.concatenate([token_rows, grad_rows], axis=1).reshape(
        experts, capacity, features + quarter
    )
    arrived = send_rows(outgoing)
    slot_tokens = arrived[:, :, :features]
    slot_grads = arrived[:, :, features:]
    flat_tokens = slot_tokens.reshape(slots_total, -1)
    flat_grads = slot_grads.reshape(slots_total, quarter)
    gate_mat = gate_weight[0]
    up_mat = up_weight[0]
    down_mat = down_weight[0]
    feature_contract = (((1,), (1,)), ((), ()))
    gate_pre = lax.dot_general(
        gate_mat, flat_tokens, feature_contract, preferred_element_type=jnp.float32
    )
    up_pre = lax.dot_general(
        up_mat, flat_tokens, feature_contract, preferred_element_type=jnp.float32
    )
    sigmoid_gate = jax.nn.sigmoid(gate_pre)
    activated = gate_pre * sigmoid_gate
    hidden = (activated * up_pre).astype(jnp.bfloat16)
    piece = lax.all_gather(hidden, "dp", axis=0, tiled=True)
    down_rows = down_mat
    out_total = lax.dot_general(
        piece, down_rows, (((0,), (0,)), ((), ())), preferred_element_type=jnp.float32
    )
    block_grad = jnp.dot(piece, flat_grads, preferred_element_type=jnp.float32)
    down_total = block_grad
    out_total, down_total = (out_total, down_total)
    expert_out = out_total.astype(jnp.bfloat16)
    down_gradient = down_total.astype(jnp.bfloat16)
    returned = return_rows(expert_out.reshape(experts, capacity, quarter)).reshape(
        slots_total, quarter
    )
    picked = returned[positions].astype(jnp.float32) * gate_scale.reshape(-1)[:, None]
    layer_out = jnp.sum(picked.reshape(tok_rows, per_token, quarter), axis=1).astype(jnp.bfloat16)
    down_rows = down_mat
    hidden_grad = lax.psum_scatter(
        lax.dot_general(
            down_rows, flat_grads, feature_contract, preferred_element_type=jnp.float32
        ),
        "dp",
        scatter_dimension=0,
        tiled=True,
    )
    gate_grad = (
        hidden_grad * up_pre * sigmoid_gate * (1.0 + gate_pre * (1.0 - sigmoid_gate))
    ).astype(jnp.bfloat16)
    up_grad = (hidden_grad * activated).astype(jnp.bfloat16)
    gate_gradient = jnp.dot(gate_grad, flat_tokens, preferred_element_type=jnp.float32).astype(
        jnp.bfloat16
    )
    up_gradient = jnp.dot(up_grad, flat_tokens, preferred_element_type=jnp.float32).astype(
        jnp.bfloat16
    )
    return (layer_out, gate_gradient[None], up_gradient[None], down_gradient[None])


def solution(mesh):
    return jax.shard_map(
        body,
        mesh=mesh,
        in_specs=(
            P(("grp", "loc"), "dp"),
            P(("grp", "loc"), "dp"),
            P(("grp", "loc"), None),
            P(("grp", "loc"), None),
            P(("grp", "loc"), "dp", None),
            P(("grp", "loc"), "dp", None),
            P(("grp", "loc"), None, "dp"),
        ),
        out_specs=(
            P(("grp", "loc"), "dp"),
            P(("grp", "loc"), "dp", None),
            P(("grp", "loc"), "dp", None),
            P(("grp", "loc"), None, "dp"),
        ),
        check_vma=False,
    )
```

profile of v0, /device:TPU:1, one launch (start us, length us, event | category | flops | bytes accessed | tf_op | source)
XLA Modules:
  0.0 404.9 jit_solution(12513130628628026120)
XLA Ops:
  7.2 0.0 copy-start
  7.2 0.0 all-gather.2.cloned.1.call-start
  7.2 0.9 copy.24
  8.1 0.1 eq.29
  8.2 0.1 eq.26
  8.3 0.1 copy.27
  8.4 0.8 copy.30
  9.2 0.1 reshape.110
  9.3 0.2 fusion.19
  9.6 0.1 add_add_fusion
  9.7 0.2 fusion.18
  9.9 0.1 reduce_sum.32
  10.0 0.1 copy.29
  10.1 0.1 mul.62
  10.2 0.2 convert_reduce_fusion
  10.5 11.5 %all_gather.6 = bf16[128,2048]{1,0:T(8,128)(2,1)S(1)} all-gather(bf16[128,512]{1,0:T(8,128)(2,1)} %param.7), channel_id=1, replica_groups=mesh['dp'=4,'grp'=4,'loc'=32] {'dp'}, dimensions={1}, use_global_device_ids=true | all-gather | bytes 655360 | tf_op jit(solution)/shard_map/all_gather | solution.py:41
  21.9 3.2 convolution_convert_fusion
  25.1 2.4 scatter_custom_fusion
  27.6 0.0 copy-done.2
  27.6 0.4 multiply_convert_fusion
  28.0 2.6 maximum_bitcast_fusion
  30.6 0.0 copy-start.4
  30.6 257.2 %all_to_all.10 = bf16[128,8,2560]{2,1,0:T(8,128)(2,1)S(1)} all-to-all(bf16[128,8,2560]{2,1,0:T(8,128)(2,1)S(1)} %maximum_bitcast_fusion), channel_id=1, replica_groups=mesh['dp'=4,'grp'=4,'loc'=32] {'grp','loc'}, dimensions={0} | all-to-all | bytes 10485760 | tf_op jit(solution)/shard_map/all_to_all | solution.py:23
  287.8 0.0 copy-done.4
  287.8 1.5 fusion.10
  289.3 0.8 copy-done.1
  290.1 0.0 copy-done.5
  290.1 2.5 multiply_convert_fusion.3
  292.7 0.0 copy-done.7
  292.7 0.0 all-gather.2.cloned.1.call-update
  292.7 0.0 reduce-scatter.2.cloned.1.call-start
  292.8 0.0 copy-done
  292.8 3.9 convolution_bitcast_fusion
  296.7 0.0 reduce-scatter.2.cloned.1.call-update
  296.7 23.2 %all-gather.2.cloned.1.call-done = bf16[768,1024]{1,0:T(8,128)(2,1)} async-done(((bf16[192,1024]{1,0:T(8,128)(2,1)}), bf16[768,1024]{1,0:T(8,128)(2,1)}) %all-gather.2.cloned.1.call-update) | async-done | bytes 1572880 | tf_op jit(solution)/shard_map/all_gather | solution.py:67
  319.8 3.5 fusion.8
  323.4 16.6 %all-to-all-start.1 = ((bf16[128,8,512]{2,1,0:T(8,128)(2,1)}), bf16[128,8,512]{2,1,0:T(8,128)(2,1)S(1)}, u32[]{:S(2)}, u32[]{:S(2)}) async-start(bf16[128,8,512]{2,1,0:T(8,128)(2,1)} %fusion.8), calls=%async_computation.1 | async-start | bytes 2097152 | tf_op jit(solution)/shard_map/all_to_all | solution.py:27
  340.0 0.0 copy-done.3
  340.0 3.1 fusion.9
  343.1 25.7 %reduce-scatter.2.cloned.1.call-done = f32[192,1024]{1,0:T(8,128)} async-done(((f32[768,1024]{1,0:T(8,128)}), f32[192,1024]{1,0:T(8,128)}) %reduce-scatter.2.cloned.1.call-update) | async-done | bytes 786448 | tf_op jit(solution)/shard_map/reduce_scatter | solution.py:83
  368.8 4.6 %fusion.6 = bf16[1,192,2048]{2,1,0:T(8,128)(2,1)} fusion(bf16[128,8,2560]{2,1,0:T(8,128)(2,1)} %copy-done.1, f32[192,1024]{1,0:T(8,128)} %reduce-scatter.2.cloned.1.call-done, f32[192,1024]{1,0:T(8,128)} %copy-done.7), kind=kOutput, calls=%fused_computation.11 | convolution fusion | flops 806879232 | bytes 6553600 | tf_op jit(solution)/shard_map/dot_general | solution.py:98
  373.5 0.0 copy-done.8
  373.5 0.0 copy-done.9
  373.5 4.2 %fusion.7 = bf16[1,192,2048]{2,1,0:T(8,128)(2,1)} fusion(bf16[128,8,2560]{2,1,0:T(8,128)(2,1)} %copy-done.1, f32[192,1024]{1,0:T(8,128)S(1)} %copy-done.8, f32[192,1024]{1,0:T(8,128)S(1)} %copy-done.6, f32[192,1024]{1,0:T(8,128)S(1)} %copy-done.9), kind=kOutput, calls=%fused_computation.12 | convolution fusion | flops 807665664 | bytes 7340032 | tf_op jit(solution)/shard_map/dot_general | solution.py:95
  377.7 16.6 %all-to-all-done.1 = bf16[128,8,512]{2,1,0:T(8,128)(2,1)S(1)} async-done(((bf16[128,8,512]{2,1,0:T(8,128)(2,1)}), bf16[128,8,512]{2,1,0:T(8,128)(2,1)S(1)}, u32[]{:S(2)}, u32[]{:S(2)}) %all-to-all-start.1) | async-done | bytes 1048608 | tf_op jit(solution)/shard_map/all_to_all | solution.py:27
  394.4 2.0 gather_fusion
  396.3 0.3 reshape.97
  396.7 1.4 multiply_reduce_fusion
  (16 shorter events, 0.1 us)
Async XLA Ops:
  7.2 285.6 %copy-start = (bf16[1,768,512]{2,1,0:T(8,128)(2,1)S(1)}, bf16[1,768,512]{2,1,0:T(8,128)(2,1)}, u32[]{:S(2)}) copy-start(bf16[1,768,512]{2,1,0:T(8,128)(2,1)} %param.13) | copy-start | bytes 2359300
  7.2 312.7 %all-gather.2.cloned.1.call-start = ((), (), s32[]{:S(2)}) async-start(), calls=%async_computation.3 | async-start | bytes 1966080 | tf_op jit(solution)/shard_map/all_gather | solution.py:67
  21.9 5.6 %copy-start.2 = (bf16[128,512]{1,0:T(8,128)(2,1)S(1)}, bf16[128,512]{1,0:T(8,128)(2,1)}, u32[]{:S(2)}) copy-start(bf16[128,512]{1,0:T(8,128)(2,1)} %param.8) | copy-start | bytes 393220
  30.6 257.2 %copy-start.4 = (bf16[1,192,2048]{2,1,0:T(8,128)(2,1)S(1)}, bf16[1,192,2048]{2,1,0:T(8,128)(2,1)}, u32[]{:S(2)}) copy-start(bf16[1,192,2048]{2,1,0:T(8,128)(2,1)} %param.11) | copy-start | bytes 2359300
  287.8 2.3 copy-start.1
  287.8 2.3 copy-start.5
  290.1 2.5 copy-start.7
  292.7 76.1 %reduce-scatter.2.cloned.1.call-start = ((), (), s32[]{:S(2)}) async-start(), calls=%async_computation.4 | async-start | bytes 3932160 | tf_op jit(solution)/shard_map/reduce_scatter | solution.py:83
  319.8 20.2 %copy-start.3 = (bf16[768,1024]{1,0:T(8,128)(2,1)S(1)}, bf16[768,1024]{1,0:T(8,128)(2,1)}, u32[]{:S(2)}) copy-start(bf16[768,1024]{1,0:T(8,128)(2,1)} %all-gather.2.cloned.1.call-done) | copy-start | bytes 4718596
  323.4 71.0 %all-to-all-start.1 = ((bf16[128,8,512]{2,1,0:T(8,128)(2,1)}), bf16[128,8,512]{2,1,0:T(8,128)(2,1)S(1)}, u32[]{:S(2)}, u32[]{:S(2)}) async-start(bf16[128,8,512]{2,1,0:T(8,128)(2,1)} %fusion.8), calls=%async_computation.1 | async-start | bytes 2097152 | tf_op jit(solution)/shard_map/all_to_all | solution.py:27
  343.1 30.3 %copy-start.8 = (f32[192,1024]{1,0:T(8,128)S(1)}, f32[192,1024]{1,0:T(8,128)}, u32[]{:S(2)}) copy-start(f32[192,1024]{1,0:T(8,128)} %copy-done.7) | copy-start | bytes 2359300
  343.1 30.3 %copy-start.9 = (f32[192,1024]{1,0:T(8,128)S(1)}, f32[192,1024]{1,0:T(8,128)}, u32[]{:S(2)}) copy-start(f32[192,1024]{1,0:T(8,128)} %get-tuple-element.7) | copy-start | bytes 2359300
  368.8 4.6 %copy-start.6 = (f32[192,1024]{1,0:T(8,128)S(1)}, f32[192,1024]{1,0:T(8,128)}, u32[]{:S(2)}) copy-start(f32[192,1024]{1,0:T(8,128)} %reduce-scatter.2.cloned.1.call-done) | copy-start | bytes 2359300
Sparse Core Ops, SparseCore 0:
  292.8 26.9 all-gather.1
  322.7 46.1 reduce-scatter.1
where the time goes:
time: 406 us; the launch traced here: 405 us
  blocking collectives  269 us (66%)
  waiting for transfers between devices  65.5 us (16%)
  matrix products  27.1 us (7%)
  starting transfers between devices  16.7 us (4%)
  between operations  14.2 us (3%)
  local copies, waits for them, and re-layouts  7.97 us (2%)
  other arithmetic  4.76 us (1%)
    all_to_all x1, blocking collectives, send_rows(): lax.all_to_all(outgoing, ('grp', 'loc'), split_axis=0, concat_axis=0, til...  257 us
    reduce_scatter x1, waiting for transfers between devices, body(): lax.psum_scatter(lax.dot_general(down_rows, flat_grads, feature_contract,...  25.7 us
    all_gather x1, waiting for transfers between devices, body(): piece = lax.all_gather(hidden, 'dp', axis=0, tiled=True)  23.2 us
    all_to_all x1, waiting for transfers between devices, return_rows(): lax.all_to_all(results, ('grp', 'loc'), split_axis=0, concat_axis=0, tile...  16.6 us
    all_to_all x1, starting transfers between devices, return_rows(): lax.all_to_all(results, ('grp', 'loc'), split_axis=0, concat_axis=0, tile...  16.6 us
    all_gather x1, blocking collectives, body(): full_tokens = lax.all_gather(tokens, 'dp', axis=1, tiled=True)  11.5 us
  transfers between devices with their start and end apart: 3, of which 3 were waited for; matrix products, arithmetic and copies ran while one was open for 5% of the time, Pallas kernels for 0%

commit v1 on v0

--- a/solution.py
+++ b/solution.py
@@ -38,19 +38,15 @@
     slot_scale = jnp.zeros((slots_total,), jnp.float32).at[positions].set(gate_scale.reshape(-1))
     picked_grads = jnp.dot(unit_place, grad_out, preferred_element_type=jnp.float32)
     grad_rows = (picked_grads * slot_scale[:, None]).astype(jnp.bfloat16)
-    full_tokens = lax.all_gather(tokens, "dp", axis=1, tiled=True)
-    features = full_tokens.shape[1]
-    token_rows = jnp.dot(unit_place, full_tokens, preferred_element_type=jnp.float32).astype(
+    token_rows = jnp.dot(unit_place, tokens, preferred_element_type=jnp.float32).astype(
         jnp.bfloat16
     )
     outgoing = jnp.concatenate([token_rows, grad_rows], axis=1).reshape(
-        experts, capacity, features + quarter
+        experts, capacity, 2 * quarter
     )
-    arrived = send_rows(outgoing)
-    slot_tokens = arrived[:, :, :features]
-    slot_grads = arrived[:, :, features:]
-    flat_tokens = slot_tokens.reshape(slots_total, -1)
-    flat_grads = slot_grads.reshape(slots_total, quarter)
+    arrived = send_rows(outgoing).reshape(slots_total, 2 * quarter)
+    flat_grads = arrived[:, quarter:]
+    flat_tokens = lax.all_gather(arrived[:, :quarter], "dp", axis=1, tiled=True)
     gate_mat = gate_weight[0]
     up_mat = up_weight[0]
     down_mat = down_weight[0]

time: 406 us -> 316 us (0.78)
  blocking collectives: 269 us -> 120 us
  waiting for transfers between devices: 65.5 us -> 128 us
    all_to_all x1, blocking collectives: 257 us -> 120 us  [send_rows(): lax.all_to_all(outgoing, ('grp', 'loc'), split_axis=0, concat_axis=0, til...]
    all_gather x0 -> x1, waiting for transfers between devices: none -> 49.7 us  [body(): flat_tokens = lax.all_gather(arrived[:, :quarter], 'dp', axis=1, tiled=True)]
    all_gather x1 -> x0, blocking collectives: 11.5 us -> none  [body(): full_tokens = lax.all_gather(tokens, 'dp', axis=1, tiled=True)]
    all_gather x1, waiting for transfers between devices: 23.2 us -> 32 us  [body(): piece = lax.all_gather(hidden, 'dp', axis=0, tiled=True)]
  transfers between devices with their start and end apart: 3 -> 4, of which waited for: 3 -> 4; matrix products, arithmetic and copies ran while one was open for 5% -> 5% of each run, Pallas kernels for 0% -> 0%
where the time goes in v1:
time: 316 us; the launch traced here: 315 us
  waiting for transfers between devices  128 us (41%)
  blocking collectives  120 us (38%)
  matrix products  23.1 us (7%)
  starting transfers between devices  16.9 us (5%)
  between operations  14 us (4%)
  local copies, waits for them, and re-layouts  11.7 us (4%)
    all_to_all x1, blocking collectives, send_rows(): lax.all_to_all(outgoing, ('grp', 'loc'), split_axis=0, concat_axis=0, til...  120 us
    all_gather x1, waiting for transfers between devices, body(): flat_tokens = lax.all_gather(arrived[:, :quarter], 'dp', axis=1, tiled=True)  49.7 us
    all_gather x1, waiting for transfers between devices, body(): piece = lax.all_gather(hidden, 'dp', axis=0, tiled=True)  32 us
    reduce_scatter x1, waiting for transfers between devices, body(): lax.psum_scatter(lax.dot_general(down_rows, flat_grads, feature_contract,...  28.8 us
    all_to_all x1, waiting for transfers between devices, return_rows(): lax.all_to_all(results, ('grp', 'loc'), split_axis=0, concat_axis=0, tile...  17 us
    all_to_all x1, starting transfers between devices, return_rows(): lax.all_to_all(results, ('grp', 'loc'), split_axis=0, concat_axis=0, tile...  16.7 us
  transfers between devices with their start and end apart: 4, of which 4 were waited for; matrix products, arithmetic and copies ran while one was open for 5% of the time, Pallas kernels for 0%

profile of v1, /device:TPU:1, one launch (start us, length us, event | category | flops | bytes accessed | tf_op | source)
XLA Modules:
  0.0 315.1 jit_solution(664736426961336198)
XLA Ops:
  7.2 0.0 copy-start
  7.2 0.0 all-gather.3.cloned.1.call-start
  7.2 0.9 copy.23
  8.1 0.1 eq.29
  8.2 0.1 eq.26
  8.3 0.1 copy.26
  8.4 0.8 copy.29
  9.2 0.1 reshape.106
  9.3 0.2 fusion.13
  9.6 0.1 add_add_fusion
  9.7 0.2 fusion.12
  9.9 0.1 reduce_sum.32
  10.1 0.1 copy.28
  10.1 0.1 mul.62
  10.2 0.2 convert_reduce_fusion
  10.5 1.5 convolution_convert_fusion.3
  12.0 2.4 scatter_custom_fusion
  14.4 0.5 multiply_convert_fusion
  14.9 0.7 copy-done.3
  15.7 0.2 pad_maximum_fusion
  15.8 2.6 copy.30
  18.4 119.5 %all_to_all.10 = bf16[128,8,1024]{2,1,0:T(8,128)(2,1)S(1)} all-to-all(bf16[128,8,1024]{2,1,0:T(8,128)(2,1)} %bitcast.55), channel_id=1, replica_groups=mesh['dp'=4,'grp'=4,'loc'=32] {'grp','loc'}, dimensions={0} | all-to-all | bytes 4194304 | tf_op jit(solution)/shard_map/all_to_all | solution.py:23
  137.9 1.2 slice.19
  139.1 0.0 all-gather.3.cloned.1.call-update
  139.2 0.0 all-gather.5.cloned.1.call-start
  139.2 49.7 %all-gather.3.cloned.1.call-done = bf16[1024,2048]{1,0:T(8,128)(2,1)} async-done(((bf16[1024,512]{1,0:T(8,128)(2,1)}), bf16[1024,2048]{1,0:T(8,128)(2,1)}) %all-gather.3.cloned.1.call-update) | async-done | bytes 4194320 | tf_op jit(solution)/shard_map/all_gather | solution.py:49
  188.9 4.1 %convolution_bitcast_fusion.2 = f32[192,1024]{1,0:T(8,128)S(1)} fusion(bf16[1024,2048]{1,0:T(8,128)(2,1)} %all-gather.3.cloned.1.call-done, bf16[1,192,2048]{2,1,0:T(8,128)(2,1)} %param.11), kind=kOutput, calls=%fused_computation.17 | convolution fusion | flops 805306368 | bytes 5767168 | tf_op jit(solution)/shard_map/dot_general | solution.py:54
  193.0 0.0 copy-start.11
  193.0 2.6 multiply_convert_fusion.3
  195.5 0.0 copy-done.11
  195.5 0.0 all-gather.5.cloned.1.call-update
  195.6 0.0 reduce-scatter.2.cloned.1.call-start
  195.6 2.7 convolution_bitcast_fusion
  198.4 0.0 reduce-scatter.2.cloned.1.call-update
  198.4 32.0 %all-gather.5.cloned.1.call-done = bf16[768,1024]{1,0:T(8,128)(2,1)} async-done(((bf16[192,1024]{1,0:T(8,128)(2,1)}), bf16[768,1024]{1,0:T(8,128)(2,1)}) %all-gather.5.cloned.1.call-update) | async-done | bytes 1572880 | tf_op jit(solution)/shard_map/all_gather | solution.py:63
  230.4 3.4 %fusion.2 = bf16[128,8,512]{2,1,0:T(8,128)(2,1)} fusion(bf16[768,1024]{1,0:T(8,128)(2,1)} %all-gather.5.cloned.1.call-done, bf16[1,768,512]{2,1,0:T(8,128)(2,1)S(1)} %copy-done), kind=kOutput, calls=%fused_computation.14 | convolution fusion | flops 805830656 | bytes 3407872 | tf_op jit(solution)/shard_map/dot_general | solution.py:65
  233.8 16.7 %all-to-all-start.1 = ((bf16[128,8,512]{2,1,0:T(8,128)(2,1)}), bf16[128,8,512]{2,1,0:T(8,128)(2,1)S(1)}, u32[]{:S(2)}, u32[]{:S(2)}) async-start(bf16[128,8,512]{2,1,0:T(8,128)(2,1)} %fusion.2), calls=%async_computation.1 | async-start | bytes 2097152 | tf_op jit(solution)/shard_map/all_to_all | solution.py:27
  250.6 0.0 copy-start.13
  250.6 28.8 %reduce-scatter.2.cloned.1.call-done = f32[192,1024]{1,0:T(8,128)} async-done(((f32[768,1024]{1,0:T(8,128)}), f32[192,1024]{1,0:T(8,128)}) %reduce-scatter.2.cloned.1.call-update) | async-done | bytes 786448 | tf_op jit(solution)/shard_map/reduce_scatter | solution.py:79
  279.4 4.5 %fusion.1 = bf16[1,192,2048]{2,1,0:T(8,128)(2,1)} fusion(bf16[1024,2048]{1,0:T(8,128)(2,1)} %all-gather.3.cloned.1.call-done, f32[192,1024]{1,0:T(8,128)} %reduce-scatter.2.cloned.1.call-done, f32[192,1024]{1,0:T(8,128)S(1)} %copy-done.12), kind=kOutput, calls=%fused_computation.5 | convolution fusion | flops 806879232 | bytes 6553600 | tf_op jit(solution)/shard_map/dot_general | solution.py:94
  283.9 0.0 copy-done.7
  283.9 2.1 fusion
  286.0 0.0 copy-done.8
  286.0 1.9 fusion.3
  287.9 17.0 %all-to-all-done.1 = bf16[128,8,512]{2,1,0:T(8,128)(2,1)S(1)} async-done(((bf16[128,8,512]{2,1,0:T(8,128)(2,1)}), bf16[128,8,512]{2,1,0:T(8,128)(2,1)S(1)}, u32[]{:S(2)}, u32[]{:S(2)}) %all-to-all-start.1) | async-done | bytes 1048608 | tf_op jit(solution)/shard_map/all_to_all | solution.py:27
  304.9 2.0 gather_fusion
  306.9 0.3 reshape.93
  307.2 1.4 multiply_reduce_fusion
  (28 shorter events, 0.1 us)
Async XLA Ops:
  7.2 188.5 %copy-start = (bf16[1,768,512]{2,1,0:T(8,128)(2,1)S(1)}, bf16[1,768,512]{2,1,0:T(8,128)(2,1)}, u32[]{:S(2)}) copy-start(bf16[1,768,512]{2,1,0:T(8,128)(2,1)} %param.13) | copy-start | bytes 2359300
  7.2 3.3 %copy-start.4 = (bf16[128,512]{1,0:T(8,128)(2,1)S(1)}, bf16[128,512]{1,0:T(8,128)(2,1)}, u32[]{:S(2)}) copy-start(bf16[128,512]{1,0:T(8,128)(2,1)} %param.7) | copy-start | bytes 393220
  7.2 181.7 %all-gather.3.cloned.1.call-start = ((), (), s32[]{:S(2)}) async-start(), calls=%async_computation.3 | async-start | bytes 5242880 | tf_op jit(solution)/shard_map/all_gather | solution.py:49
  8.1 6.3 %copy-start.5 = (bf16[128,512]{1,0:T(8,128)(2,1)S(1)}, bf16[128,512]{1,0:T(8,128)(2,1)}, u32[]{:S(2)}) copy-start(bf16[128,512]{1,0:T(8,128)(2,1)} %param.8) | copy-start | bytes 393220
  14.4 1.2 copy-start.3
  137.9 57.7 %copy-start.1 = (bf16[128,8,1024]{2,1,0:T(8,128)(2,1)}, bf16[128,8,1024]{2,1,0:T(8,128)(2,1)S(1)}, u32[]{:S(2)}) copy-start(bf16[128,8,1024]{2,1,0:T(8,128)(2,1)S(1)} %all_to_all.10) | copy-start | bytes 6291460
  139.2 91.2 %all-gather.5.cloned.1.call-start = ((), (), s32[]{:S(2)}) async-start(), calls=%async_computation.4 | async-start | bytes 1966080 | tf_op jit(solution)/shard_map/all_gather | solution.py:63
  188.9 4.1 %copy-start.6 = (bf16[1024,2048]{1,0:T(8,128)(2,1)S(1)}, bf16[1024,2048]{1,0:T(8,128)(2,1)}, u32[]{:S(2)}) copy-start(bf16[1024,2048]{1,0:T(8,128)(2,1)} %all-gather.3.cloned.1.call-done) | copy-start | bytes 12582916
  188.9 4.1 %copy-start.9 = (bf16[1,192,2048]{2,1,0:T(8,128)(2,1)S(1)}, bf16[1,192,2048]{2,1,0:T(8,128)(2,1)}, u32[]{:S(2)}) copy-start(bf16[1,192,2048]{2,1,0:T(8,128)(2,1)} %param.12) | copy-start | bytes 2359300
  193.0 2.6 copy-start.11
  195.6 83.8 %reduce-scatter.2.cloned.1.call-start = ((), (), s32[]{:S(2)}) async-start(), calls=%async_computation.5 | async-start | bytes 3932160 | tf_op jit(solution)/shard_map/reduce_scatter | solution.py:79
  233.8 45.6 %copy-start.12 = (f32[192,1024]{1,0:T(8,128)S(1)}, f32[192,1024]{1,0:T(8,128)}, u32[]{:S(2)}) copy-start(f32[192,1024]{1,0:T(8,128)} %copy-done.11) | copy-start | bytes 2359300
  233.8 71.1 %all-to-all-start.1 = ((bf16[128,8,512]{2,1,0:T(8,128)(2,1)}), bf16[128,8,512]{2,1,0:T(8,128)(2,1)S(1)}, u32[]{:S(2)}, u32[]{:S(2)}) async-start(bf16[128,8,512]{2,1,0:T(8,128)(2,1)} %fusion.2), calls=%async_computation.1 | async-start | bytes 2097152 | tf_op jit(solution)/shard_map/all_to_all | solution.py:27
  250.6 33.4 %copy-start.13 = (f32[192,1024]{1,0:T(8,128)S(1)}, f32[192,1024]{1,0:T(8,128)}, u32[]{:S(2)}) copy-start(f32[192,1024]{1,0:T(8,128)} %get-tuple-element.7) | copy-start | bytes 2359300
  279.4 4.5 %copy-start.7 = (bf16[1024,2048]{1,0:T(8,128)(2,1)S(1)}, bf16[1024,2048]{1,0:T(8,128)(2,1)}, u32[]{:S(2)}) copy-start(bf16[1024,2048]{1,0:T(8,128)(2,1)} %all-gather.3.cloned.1.call-done) | copy-start | bytes 12582916
  279.4 4.5 %copy-start.10 = (f32[192,1024]{1,0:T(8,128)S(1)}, f32[192,1024]{1,0:T(8,128)}, u32[]{:S(2)}) copy-start(f32[192,1024]{1,0:T(8,128)} %reduce-scatter.2.cloned.1.call-done) | copy-start | bytes 2359300
  283.9 2.1 copy-start.2
  283.9 2.1 copy-start.8
Sparse Core Ops, SparseCore 0:
  139.3 49.5 all-gather.2
  195.7 34.6 all-gather.4
  233.2 46.1 reduce-scatter.1

commit v2 on v1

v2 whole, which is shorter than its diff:
```python
import functools

import jax
import jax.numpy as jnp
from jax import lax
from jax.experimental import pallas as pl
from jax.experimental.pallas import tpu as pltpu
from jax.sharding import PartitionSpec as P

MESH = pl.DeviceIdType.MESH
CAP = 8
PAIR = 2 * CAP


def slot_layout(route_ids, experts, capacity):
    flat_ids = route_ids.reshape(-1)
    onehot = (
        flat_ids[:, None] == lax.broadcasted_iota(jnp.int32, (flat_ids.shape[0], experts), 1)
    ).astype(jnp.int32)
    ranks = jnp.sum((jnp.cumsum(onehot, axis=0) - 1) * onehot, axis=1)
    return flat_ids * capacity + ranks


def route_rows(ids, scale, plane_experts, planes):
    rows, per_token = ids.shape
    experts = plane_experts * planes
    expert_lane = lax.broadcasted_iota(jnp.int32, (rows, experts), 1)
    hits = [ids[:, k : k + 1] == expert_lane for k in range(per_token)]
    named = sum(h.astype(jnp.float32) for h in hits).astype(jnp.bfloat16)
    row_at = lax.broadcasted_iota(jnp.int32, (rows, rows), 0)
    col_at = lax.broadcasted_iota(jnp.int32, (rows, rows), 1)
    earlier = (col_at < row_at).astype(jnp.float32).astype(jnp.bfloat16)
    before = jnp.dot(earlier, named, preferred_element_type=jnp.float32)
    lane = lax.broadcasted_iota(jnp.int32, (rows, rows), 1)
    table = jnp.zeros((rows, rows), jnp.float32)
    loc_size = 2 * planes
    for k in range(per_token):
        rank = jnp.sum(jnp.where(hits[k], before, 0.0), axis=1, keepdims=True)
        e = ids[:, k : k + 1]
        group = lax.div(e, jnp.int32(loc_size))
        local = e - group * loc_size
        plane = lax.div(local, jnp.int32(2))
        member = group * 2 + (local - plane * 2)
        key = (plane * (plane_experts * PAIR) + member * PAIR).astype(jnp.float32) + rank
        table = jnp.where(lane == k, key, table)
        table = jnp.where(lane == per_token + k, scale[:, k : k + 1], table)
    return table.T[0 : 2 * per_token, :]


def dispatch_kernel(
    nx, nz, ids_ref, scale_ref, tok_ref, grad_ref, otok_ref, ograd_ref,
    zt, zg, zm, xt, xg, slot_t, slot_g,
    z_send, z_recv, x_send, x_recv, y_send, y_recv, l_sem,
):
    R = nz // 2
    J = 2 * nx
    per_token = ids_ref.shape[1]
    y = lax.axis_index("dp")
    x = lax.axis_index("grp")
    loc = lax.axis_index("loc")
    z = loc // 2
    core = loc % 2
    me = x * 2 + core
    z_right = {"loc": ((z + 1) % nz) * 2 + core}
    z_left = {"loc": ((z + nz - 1) % nz) * 2 + core}
    yp, ym, yo = (y + 1) % 4, (y + 3) % 4, (y + 2) % 4
    y_up, y_down = {"dp": yp}, {"dp": ym}

    def plane_device(j):
        return {"grp": j // 2, "loc": z * 2 + j % 2}

    barrier = pltpu.get_barrier_semaphore()
    greeted = [z_right, z_left, y_up, y_down]
    greeted += [plane_device((me + o) % J) for o in range(1, J)]
    for device in greeted:
        pl.semaphore_signal(barrier, inc=1, device_id=device, device_id_type=MESH)

    zt[0, 0] = tok_ref[...]
    zg[0, 0] = grad_ref[...]
    zm[0, 0] = route_rows(ids_ref[...], scale_ref[...], J, nz)
    pl.semaphore_wait(barrier, len(greeted))

    bufs = (zt, zg, zm)

    def z_copy(kind, way, step, src, dst):
        return pltpu.make_async_remote_copy(
            src_ref=bufs[kind].at[src],
            dst_ref=bufs[kind].at[dst],
            send_sem=z_send.at[way, step, kind],
            recv_sem=z_recv.at[dst[0], dst[1], kind],
            device_id=z_right if way == 0 else z_left,
            device_id_type=MESH,
        )

    def x_copy(kind, i, o):
        j = (me + o) % J
        src, dst = ((xt, slot_t.at[y]), (xg, slot_g))[kind]
        return pltpu.make_async_remote_copy(
            src_ref=src.at[i, j],
            dst_ref=dst.at[i, me],
            send_sem=x_send.at[i, kind, o],
            recv_sem=x_recv.at[i, kind, o],
            device_id=plane_device(j),
            device_id_type=MESH,
        )

    def x_own(kind, i):
        src, dst = ((xt, slot_t.at[y]), (xg, slot_g))[kind]
        return pltpu.make_async_copy(src.at[i, me], dst.at[i, me], x_recv.at[i, kind, 0])

    def y_copy(k, i):
        ref = (
            slot_t.at[y, i],
            slot_t.at[y, i],
            slot_t.at[ym, i, pl.ds(0, J // 2)],
            slot_t.at[yp, i, pl.ds(J // 2, J // 2)],
        )[k]
        return pltpu.make_async_remote_copy(
            src_ref=ref,
            dst_ref=ref,
            send_sem=y_send.at[i, k],
            recv_sem=y_recv.at[i, k],
            device_id=y_up if k % 2 == 0 else y_down,
            device_id_type=MESH,
        )

    def y_arrival(k, i):
        ref = (
            slot_t.at[ym, i],
            slot_t.at[yp, i],
            slot_t.at[yo, i, pl.ds(0, J // 2)],
            slot_t.at[yo, i, pl.ds(J // 2, J // 2)],
        )[k]
        return pltpu.make_async_remote_copy(
            src_ref=ref,
            dst_ref=ref,
            send_sem=y_send.at[i, k],
            recv_sem=y_recv.at[i, k],
            device_id=y_up if k % 2 == 0 else y_down,
            device_id_type=MESH,
        )

    def select(i):
        marks, weights = [], 0.0
        for h in range(2):
            row_key = (
                lax.broadcasted_iota(jnp.int32, (J * PAIR, zm.shape[3]), 0)
                + (z * (J * PAIR) - h * CAP)
            ).astype(jnp.float32)
            table = zm[i, h]
            mark = 0.0
            for k in range(per_token):
                hit = table[k : k + 1, :] == row_key
                mark = mark + jnp.where(hit, 1.0, 0.0)
                weights = weights + jnp.where(hit, table[per_token + k : per_token + k + 1, :], 0.0)
            marks.append(mark)
        place = jnp.concatenate(marks, axis=1).astype(jnp.bfloat16)
        row_scale = jnp.sum(weights, axis=1, keepdims=True)
        Q = zt.shape[3]
        picked = jnp.dot(
            place, zt[i].reshape(-1, Q), preferred_element_type=jnp.float32
        )
        xt[i] = picked.astype(jnp.bfloat16).reshape(J, PAIR, Q)
        picked_g = jnp.dot(
            place, zg[i].reshape(-1, Q), preferred_element_type=jnp.float32
        )
        xg[i] = (picked_g * row_scale).astype(jnp.bfloat16).reshape(J, PAIR, Q)

    def z_stage(i):
        @pl.when(i >= 1)
        def _():
            for kind in (0, 2):
                z_copy(kind, 1, 0, (i, 0), (i, 0)).wait_recv()

        @pl.when(i < R - 1)
        def _():
            for kind in (0, 2):
                z_copy(kind, 1, i, (i, 0), (i + 1, 0)).start()

        for kind in (0, 2):
            z_copy(kind, 0, 0, (i, 1), (i, 1)).wait_recv()

        @pl.when(i < R - 1)
        def _():
            for kind in (0, 2):
                z_copy(kind, 0, i + 1, (i, 1), (i + 1, 1)).start()

        @pl.when(i >= 1)
        def _():
            z_copy(1, 1, 0, (i, 0), (i, 0)).wait_recv()

        @pl.when(i < R - 1)
        def _():
            z_copy(1, 1, i, (i, 0), (i + 1, 0)).start()

        @pl.when(i == R - 1)
        def _():
            z_copy(1, 1, R - 1, (R - 1, 0), (R - 1, 1)).start()

        z_copy(1, 0, 0, (i, 1), (i, 1)).wait_recv()

        @pl.when(i < R - 2)
        def _():
            z_copy(1, 0, i + 1, (i, 1), (i + 1, 1)).start()

        select(i)
        for kind in (0, 1):
            x_own(kind, i).start()
            for o in range(1, J):
                x_copy(kind, i, o).start()

    def x_arrival(kind, i, o):
        src, dst = ((xt, slot_t.at[y]), (xg, slot_g))[kind]
        return pltpu.make_async_remote_copy(
            src_ref=src.at[i, 0],
            dst_ref=dst.at[i, (me + J - o) % J],
            send_sem=x_send.at[i, kind, o],
            recv_sem=x_recv.at[i, kind, o],
            device_id=plane_device((me + o) % J),
            device_id_type=MESH,
        )

    def x_stage(i):
        x_own(0, i).wait()
        for o in range(1, J):
            x_arrival(0, i, o).wait_recv()
        y_copy(0, i).start()
        y_copy(1, i).start()
        x_own(1, i).wait()
        for o in range(1, J):
            x_arrival(1, i, o).wait_recv()

    def y_stage(i):
        y_arrival(0, i).wait_recv()
        y_copy(2, i).start()
        y_arrival(1, i).wait_recv()
        y_copy(3, i).start()

    def last_stage(i):
        y_arrival(2, i).wait_recv()
        y_arrival(3, i).wait_recv()

    for kind in (0, 2, 1):
        if kind == 1 and R == 1:
            continue
        z_copy(kind, 0, 0, (0, 0), (0, 1)).start()

    def step(i, carry):
        @pl.when(i < R)
        def _():
            z_stage(i)

        @pl.when((i >= 1) & (i < R + 1))
        def _():
            x_stage(i - 1)

        @pl.when((i >= 2) & (i < R + 2))
        def _():
            y_stage(i - 2)

        @pl.when(i >= 3)
        def _():
            last_stage(i - 3)

        return carry

    lax.fori_loop(0, R + 3, step, 0)

    out_t = pltpu.make_async_copy(slot_t, otok_ref, l_sem.at[0])
    out_g = pltpu.make_async_copy(slot_g, ograd_ref, l_sem.at[1])
    out_t.start()
    out_g.start()

    def drain(i, carry):
        for kind in (0, 2):
            z_copy(kind, 0, i, (0, 0), (0, 1)).wait_send()

        @pl.when(i < R - 1)
        def _():
            z_copy(1, 0, i, (0, 0), (0, 1)).wait_send()
            for kind in (0, 2):
                z_copy(kind, 1, i, (0, 0), (0, 1)).wait_send()

        z_copy(1, 1, i, (0, 0), (0, 1)).wait_send()
        for kind in (0, 1):
            for o in range(1, J):
                x_copy(kind, i, o).wait_send()
        for k in range(4):
            y_copy(k, i).wait_send()
        return carry

    lax.fori_loop(0, R, drain, 0)
    out_t.wait()
    out_g.wait()


def dispatch(ids, scale, tokens, grad_out):
    nx = lax.axis_size("grp")
    nz = lax.axis_size("loc") // 2
    rows, Q = tokens.shape
    R, J = nz // 2, 2 * nx
    bf16 = jnp.bfloat16
    vmem = pl.BlockSpec(memory_space=pltpu.VMEM)
    hbm = pl.BlockSpec(memory_space=pl.ANY)
    return pl.pallas_call(
        functools.partial(dispatch_kernel, nx, nz),
        out_shape=(
            jax.ShapeDtypeStruct((4, R, J, PAIR, Q), bf16),
            jax.ShapeDtypeStruct((R, J, PAIR, Q), bf16),
        ),
        in_specs=[vmem] * 4,
        out_specs=(hbm, hbm),
        scratch_shapes=[
            pltpu.VMEM((R, 2, rows, Q), bf16),
            pltpu.VMEM((R, 2, rows, Q), bf16),
            pltpu.VMEM((R, 2, 2 * ids.shape[1], rows), jnp.float32),
            pltpu.VMEM((R, J, PAIR, Q), bf16),
            pltpu.VMEM((R, J, PAIR, Q), bf16),
            pltpu.VMEM((4, R, J, PAIR, Q), bf16),
            pltpu.VMEM((R, J, PAIR, Q), bf16),
            pltpu.SemaphoreType.DMA((2, R, 3)),
            pltpu.SemaphoreType.DMA((R, 2, 3)),
            pltpu.SemaphoreType.DMA((R, 2, J)),
            pltpu.SemaphoreType.DMA((R, 2, J)),
            pltpu.SemaphoreType.DMA((R, 4)),
            pltpu.SemaphoreType.DMA((R, 4)),
            pltpu.SemaphoreType.DMA((2,)),
        ],
        compiler_params=pltpu.CompilerParams(
            collective_id=0, has_side_effects=True, vmem_limit_bytes=40 * 1024 * 1024
        ),
    )(ids, scale, tokens, grad_out)


def body(tokens, grad_out, expert_ids, gate_scale, gate_weight, up_weight, down_weight):
    tok_rows, quarter = tokens.shape
    per_token = expert_ids.shape[1]
    experts = lax.axis_size(("grp", "loc"))
    nx = lax.axis_size("grp")
    nz = lax.axis_size("loc") // 2
    R, J = nz // 2, 2 * nx
    slots_total = experts * CAP
    positions = slot_layout(expert_ids, experts, CAP)
    slot_t, slot_g = dispatch(expert_ids, gate_scale, tokens, grad_out)
    flat_tokens = jnp.concatenate(
        [slot_t[q].reshape(slots_total, quarter) for q in range(4)], axis=1
    )
    flat_grads = slot_g.reshape(slots_total, quarter)
    gate_mat = gate_weight[0]
    up_mat = up_weight[0]
    down_mat = down_weight[0]
    feature_contract = (((1,), (1,)), ((), ()))
    gate_pre = lax.dot_general(
        gate_mat, flat_tokens, feature_contract, preferred_element_type=jnp.float32
    )
    up_pre = lax.dot_general(
        up_mat, flat_tokens, feature_contract, preferred_element_type=jnp.float32
    )
    sigmoid_gate = jax.nn.sigmoid(gate_pre)
    activated = gate_pre * sigmoid_gate
    hidden = (activated * up_pre).astype(jnp.bfloat16)
    piece = lax.all_gather(hidden, "dp", axis=0, tiled=True)
    out_total = lax.dot_general(
        piece, down_mat, (((0,), (0,)), ((), ())), preferred_element_type=jnp.float32
    )
    block_grad = jnp.dot(piece, flat_grads, preferred_element_type=jnp.float32)
    expert_out = out_total.astype(jnp.bfloat16)
    down_gradient = block_grad.astype(jnp.bfloat16)
    z = lax.axis_index("loc") // 2
    by_round = expert_out.reshape(R, J, 2, CAP, quarter)
    by_delta = jnp.concatenate([by_round[:, :, 0], by_round[::-1, :, 1]], axis=0)
    order = (jnp.arange(nz) - z) % nz
    by_plane = by_delta[order].reshape(nz, nx, 2, CAP, quarter).transpose(1, 0, 2, 3, 4)
    returned = lax.all_to_all(
        by_plane.reshape(experts, CAP, quarter), ("grp", "loc"), 0, 0, tiled=True
    ).reshape(slots_total, quarter)
    picked = returned[positions].astype(jnp.float32) * gate_scale.reshape(-1)[:, None]
    layer_out = jnp.sum(picked.reshape(tok_rows, per_token, quarter), axis=1).astype(jnp.bfloat16)
    hidden_grad = lax.psum_scatter(
        lax.dot_general(
            down_mat, flat_grads, feature_contract, preferred_element_type=jnp.float32
        ),
        "dp",
        scatter_dimension=0,
        tiled=True,
    )
    gate_grad = (
        hidden_grad * up_pre * sigmoid_gate * (1.0 + gate_pre * (1.0 - sigmoid_gate))
    ).astype(jnp.bfloat16)
    up_grad = (hidden_grad * activated).astype(jnp.bfloat16)
    gate_gradient = jnp.dot(gate_grad, flat_tokens, preferred_element_type=jnp.float32).astype(
        jnp.bfloat16
    )
    up_gradient = jnp.dot(up_grad, flat_tokens, preferred_element_type=jnp.float32).astype(
        jnp.bfloat16
    )
    return (layer_out, gate_gradient[None], up_gradient[None], down_gradient[None])


def solution(mesh):
    return jax.shard_map(
        body,
        mesh=mesh,
        in_specs=(
            P(("grp", "loc"), "dp"),
            P(("grp", "loc"), "dp"),
            P(("grp", "loc"), None),
            P(("grp", "loc"), None),
            P(("grp", "loc"), "dp", None),
            P(("grp", "loc"), "dp", None),
            P(("grp", "loc"), None, "dp"),
        ),
        out_specs=(
            P(("grp", "loc"), "dp"),
            P(("grp", "loc"), "dp", None),
            P(("grp", "loc"), "dp", None),
            P(("grp", "loc"), None, "dp"),
        ),
        check_vma=False,
    )
```

time: 316 us -> 215 us (0.68)
  blocking collectives: 120 us -> 0 us
  Pallas kernels: 0 us -> 78 us
  waiting for transfers between devices: 128 us -> 71.9 us
  matrix products: 23.1 us -> 19.6 us
    all_to_all x1 -> x0, blocking collectives: 120 us -> none  [send_rows(): lax.all_to_all(outgoing, ('grp', 'loc'), split_axis=0, concat_axis=0, til...]
    pallas_call x0 -> x1, Pallas kernels: none -> 78 us  [dispatch(): pl.pallas_call(functools.partial(dispatch_kernel, nx, nz), out_shape=(jax...]
    all_gather x1 -> x0, waiting for transfers between devices: 49.7 us -> none  [body(): flat_tokens = lax.all_gather(arrived[:, :quarter], 'dp', axis=1, tiled=True)]
    reduce_scatter x1, waiting for transfers between devices: 28.8 us -> 21.4 us  [body(): lax.psum_scatter(lax.dot_general(down_mat, flat_grads, feature_contract,...]
    all_to_all x1, waiting for transfers between devices: 17 us -> 21.7 us  [body(): lax.all_to_all(by_plane.reshape(experts, CAP, quarter), ('grp', 'loc'), 0...]
    all_gather x1, waiting for transfers between devices: 32 us -> 28.7 us  [body(): piece = lax.all_gather(hidden, 'dp', axis=0, tiled=True)]
    dot_general x4 -> x2, matrix products: 8.04 us -> 5.08 us  [the longest x1 2.65 us: body(): lax.dot_general(down_mat, flat_grads, feature_contract, preferred_element...]
  transfers between devices with their start and end apart: 4 -> 3, of which waited for: 4 -> 3; matrix products, arithmetic and copies ran while one was open for 5% -> 9% of each run, Pallas kernels for 0% -> 0%
where the time goes in v2:
time: 215 us; the launch traced here: 214 us
  Pallas kernels  78 us (36%)
  waiting for transfers between devices  71.9 us (33%)
  matrix products  19.6 us (9%)
  starting transfers between devices  16.7 us (8%)
  between operations  14.4 us (7%)
  local copies, waits for them, and re-layouts  11.4 us (5%)
    pallas_call x1, Pallas kernels, dispatch(): pl.pallas_call(functools.partial(dispatch_kernel, nx, nz), out_shape=(jax...  78 us
    all_gather x1, waiting for transfers between devices, body(): piece = lax.all_gather(hidden, 'dp', axis=0, tiled=True)  28.7 us
    all_to_all x1, waiting for transfers between devices, body(): lax.all_to_all(by_plane.reshape(experts, CAP, quarter), ('grp', 'loc'), 0...  21.7 us
    reduce_scatter x1, waiting for transfers between devices, body(): lax.psum_scatter(lax.dot_general(down_mat, flat_grads, feature_contract,...  21.4 us
    all_to_all x1, starting transfers between devices, body(): lax.all_to_all(by_plane.reshape(experts, CAP, quarter), ('grp', 'loc'), 0...  16.6 us
    dot_general x1, matrix products, body(): jnp.dot(up_grad, flat_tokens, preferred_element_type=jnp.float32)  4.68 us
  transfers between devices with their start and end apart: 3, of which 3 were waited for; matrix products, arithmetic and copies ran while one was open for 9% of the time, Pallas kernels for 0%

profile of v2, /device:TPU:1, one launch (start us, length us, event | category | flops | bytes accessed | tf_op | source)
XLA Modules:
  0.0 214.0 jit_solution(13502491110909898028)
XLA Ops:
  7.2 0.0 copy-start
  7.2 0.0 all-gather.2.cloned.1.call-start
  7.2 0.9 copy.17.ids_ref
  8.1 0.8 copy.18.scale_ref
  8.9 0.9 copy-done.1
  9.8 0.9 copy-done.2
  10.7 78.0 %shard_map.102 = (bf16[4,8,8,16,512]{4,3,2,1,0:T(8,128)(2,1)S(1)}, bf16[8,8,16,512]{3,2,1,0:T(8,128)(2,1)S(1)}) custom-call(s32[128,4]{1,0:T(8,128)S(1)} %copy.17.ids_ref, f32[128,4]{1,0:T(8,128)S(1)} %copy.18.scale_ref, bf16[128,512]{1,0:T(8,128)(2,1)S(1)} %copy-done.1, bf16[128,512]{1,0:T(8,128)(2,1)S(1)} %copy-done.2), custom_call_target="tpu_custom_call" | custom-call | tf_op jit(solution)/shard_map/pallas_call | solution.py:305
  88.7 0.0 copy-start.12
  88.7 0.7 fusion.18
  89.4 0.0 copy-start.3
  89.4 0.0 copy-start.5
  89.4 0.0 copy-start.7
  89.4 0.0 copy-start.9
  89.4 0.4 copy-done.12
  89.8 2.1 convolution_bitcast_fusion.2
  91.9 0.0 copy-done.3
  91.9 0.0 copy-done.5
  91.9 2.5 %multiply_convert_fusion.2 = (bf16[192,1024]{1,0:T(8,128)(2,1)}, f32[192,1024]{1,0:T(8,128)}) fusion(f32[192,1024]{1,0:T(8,128)S(1)} %convolution_bitcast_fusion.2, bf16[1,192,2048]{2,1,0:T(8,128)(2,1)S(1)} %copy-done.13, bf16[1024,512]{1,0:T(8,128)(2,1)S(1)} %bitcast.69, bf16[1024,512]{1,0:T(8,128)(2,1)S(1)} %bitcast.73, ...), kind=kOutput, calls=%fused_computation.21 | convolution fusion | flops 823263232 | bytes 6946816 | tf_op jit(solution)/shard_map/dot_general | solution.py:356
  94.5 0.0 copy-done.15
  94.5 0.0 all-gather.2.cloned.1.call-update
  94.5 0.0 reduce-scatter.2.cloned.1.call-start
  94.6 2.7 %convolution_bitcast_fusion = f32[768,1024]{1,0:T(8,128)} fusion(bf16[1024,512]{1,0:T(8,128)(2,1)S(1)} %bitcast.58, bf16[1,768,512]{2,1,0:T(8,128)(2,1)S(1)} %copy-done), kind=kOutput, calls=%fused_computation.7 | convolution fusion | flops 805306368 | bytes 4980736 | tf_op jit(solution)/shard_map/dot_general | solution.py:380
  97.2 0.0 reduce-scatter.2.cloned.1.call-update
  97.3 28.7 %all-gather.2.cloned.1.call-done = bf16[768,1024]{1,0:T(8,128)(2,1)} async-done(((bf16[192,1024]{1,0:T(8,128)(2,1)}), bf16[768,1024]{1,0:T(8,128)(2,1)}) %all-gather.2.cloned.1.call-update) | async-done | bytes 1572880 | tf_op jit(solution)/shard_map/all_gather | solution.py:362
  126.0 2.4 %convolution_convert_fusion.2 = bf16[1024,512]{1,0:T(8,128)(2,1)S(1)} fusion(bf16[768,1024]{1,0:T(8,128)(2,1)} %all-gather.2.cloned.1.call-done, bf16[1,768,512]{2,1,0:T(8,128)(2,1)S(1)} %copy-done), kind=kOutput, calls=%fused_computation.8 | convolution fusion | flops 805830656 | bytes 3407872 | tf_op jit(solution)/shard_map/dot_general | solution.py:363
  128.4 0.1 slice_bitcast_fusion
  128.6 0.0 copy-start.11
  128.6 0.1 pad_maximum_fusion.1
  128.7 1.6 gather_fusion
  130.3 2.3 %copy.20 = bf16[4,16,2,8,512]{4,3,2,1,0:T(8,128)(2,1)} copy(bf16[4,16,2,8,512]{4,3,2,0,1:T(8,128)(2,1)} %bitcast.61) | data formatting | bytes 2097152 | tf_op jit(solution)/shard_map/transpose | solution.py:373
  132.5 16.6 %all-to-all-start = ((bf16[128,8,512]{2,1,0:T(8,128)(2,1)}), bf16[128,8,512]{2,1,0:T(8,128)(2,1)S(1)}, u32[]{:S(2)}, u32[]{:S(2)}) async-start(bf16[128,8,512]{2,1,0:T(8,128)(2,1)} %bitcast.62), calls=%async_computation | async-start | bytes 2097152 | tf_op jit(solution)/shard_map/all_to_all | solution.py:374
  149.2 0.1 eq.23
  149.3 0.1 eq.20
  149.4 0.1 copy.21
  149.5 0.1 mul.53
  149.6 0.1 copy.24
  149.7 0.2 fusion.10
  150.0 0.1 add_add_fusion
  150.1 0.2 fusion.9
  150.3 3.3 %fusion.2 = bf16[1,768,512]{2,1,0:T(8,128)(2,1)} fusion(bf16[768,1024]{1,0:T(8,128)(2,1)} %all-gather.2.cloned.1.call-done, bf16[1024,512]{1,0:T(8,128)(2,1)S(1)} %bitcast.59), kind=kOutput, calls=%fused_computation.10 | convolution fusion | flops 805699584 | bytes 3407872 | tf_op jit(solution)/shard_map/dot_general | solution.py:366
  153.6 21.4 %reduce-scatter.2.cloned.1.call-done = f32[192,1024]{1,0:T(8,128)} async-done(((f32[768,1024]{1,0:T(8,128)}), f32[192,1024]{1,0:T(8,128)}) %reduce-scatter.2.cloned.1.call-update) | async-done | bytes 786448 | tf_op jit(solution)/shard_map/reduce_scatter | solution.py:379
  175.0 0.0 copy-start.17
  175.0 4.7 %fusion.1 = bf16[1,192,2048]{2,1,0:T(8,128)(2,1)} fusion(f32[192,1024]{1,0:T(8,128)} %reduce-scatter.2.cloned.1.call-done, f32[192,1024]{1,0:T(8,128)} %copy-done.15, bf16[1024,512]{1,0:T(8,128)(2,1)} %bitcast.70, bf16[1024,512]{1,0:T(8,128)(2,1)} %bitcast.74, bf16[1024,512]{1,0:T(8,128)(2,1)} %bitcast.78, bf16[1024,512]{1,0:T(8,128)(2,1)} %bitcast.66), kind=kOutput, calls=%fused_computation.6 | convolution fusion | flops 823656448 | bytes 6553600 | tf_op jit(solution)/shard_map/dot_general | solution.py:394
  179.8 2.0 fusion
  181.8 21.7 %all-to-all-done = bf16[128,8,512]{2,1,0:T(8,128)(2,1)S(1)} async-done(((bf16[128,8,512]{2,1,0:T(8,128)(2,1)}), bf16[128,8,512]{2,1,0:T(8,128)(2,1)S(1)}, u32[]{:S(2)}, u32[]{:S(2)}) %all-to-all-start) | async-done | bytes 1048608 | tf_op jit(solution)/shard_map/all_to_all | solution.py:374
  203.5 2.0 gather_fusion.1
  205.5 0.3 reshape.134
  205.8 1.4 multiply_reduce_fusion
  (32 shorter events, 0.2 us)
Async XLA Ops:
  7.2 87.4 %copy-start = (bf16[1,768,512]{2,1,0:T(8,128)(2,1)S(1)}, bf16[1,768,512]{2,1,0:T(8,128)(2,1)}, u32[]{:S(2)}) copy-start(bf16[1,768,512]{2,1,0:T(8,128)(2,1)} %param.13) | copy-start | bytes 2359300
  7.2 118.8 %all-gather.2.cloned.1.call-start = ((), (), s32[]{:S(2)}) async-start(), calls=%async_computation.2 | async-start | bytes 1966080 | tf_op jit(solution)/shard_map/all_gather | solution.py:362
  8.9 0.9 copy-start.1
  9.8 0.9 copy-start.2
  88.7 1.1 copy-start.12
  89.4 2.5 %copy-start.3 = (bf16[1,8,8,16,512]{4,3,2,1,0:T(8,128)(2,1)}, bf16[1,8,8,16,512]{4,3,2,1,0:T(8,128)(2,1)S(1)}, u32[]{:S(2)}) copy-start(bf16[1,8,8,16,512]{4,3,2,1,0:T(8,128)(2,1)S(1)} %get-tuple-element.8) | copy-start | bytes 3145732
  89.4 2.5 %copy-start.5 = (bf16[1,8,8,16,512]{4,3,2,1,0:T(8,128)(2,1)}, bf16[1,8,8,16,512]{4,3,2,1,0:T(8,128)(2,1)S(1)}, u32[]{:S(2)}) copy-start(bf16[1,8,8,16,512]{4,3,2,1,0:T(8,128)(2,1)S(1)} %get-tuple-element.9) | copy-start | bytes 3145732
  89.4 2.5 %copy-start.7 = (bf16[1,8,8,16,512]{4,3,2,1,0:T(8,128)(2,1)}, bf16[1,8,8,16,512]{4,3,2,1,0:T(8,128)(2,1)S(1)}, u32[]{:S(2)}) copy-start(bf16[1,8,8,16,512]{4,3,2,1,0:T(8,128)(2,1)S(1)} %get-tuple-element.10) | copy-start | bytes 3145732
  89.4 2.5 %copy-start.9 = (bf16[1,8,8,16,512]{4,3,2,1,0:T(8,128)(2,1)}, bf16[1,8,8,16,512]{4,3,2,1,0:T(8,128)(2,1)S(1)}, u32[]{:S(2)}) copy-start(bf16[1,8,8,16,512]{4,3,2,1,0:T(8,128)(2,1)S(1)} %get-tuple-element.11) | copy-start | bytes 3145732
  89.8 2.1 copy-start.13
  91.9 2.5 %copy-start.15 = (f32[192,1024]{1,0:T(8,128)}, f32[192,1024]{1,0:T(8,128)S(1)}, u32[]{:S(2)}) copy-start(f32[192,1024]{1,0:T(8,128)S(1)} %convolution_bitcast_fusion.2) | copy-start | bytes 2359300
  94.5 80.5 %reduce-scatter.2.cloned.1.call-start = ((), (), s32[]{:S(2)}) async-start(), calls=%async_computation.3 | async-start | bytes 3932160 | tf_op jit(solution)/shard_map/reduce_scatter | solution.py:379
  128.6 20.8 %copy-start.11 = (s32[128,4]{0,1:T(4,128)S(1)}, s32[128,4]{0,1:T(4,128)}, u32[]{:S(2)}) copy-start(s32[128,4]{0,1:T(4,128)} %param.9) | copy-start | bytes 6148
  132.5 71.0 %all-to-all-start = ((bf16[128,8,512]{2,1,0:T(8,128)(2,1)}), bf16[128,8,512]{2,1,0:T(8,128)(2,1)S(1)}, u32[]{:S(2)}, u32[]{:S(2)}) async-start(bf16[128,8,512]{2,1,0:T(8,128)(2,1)} %bitcast.62), calls=%async_computation | async-start | bytes 2097152 | tf_op jit(solution)/shard_map/all_to_all | solution.py:374
  153.6 26.1 %copy-start.4 = (bf16[1,8,8,16,512]{4,3,2,1,0:T(8,128)(2,1)S(1)}, bf16[1,8,8,16,512]{4,3,2,1,0:T(8,128)(2,1)}, u32[]{:S(2)}) copy-start(bf16[1,8,8,16,512]{4,3,2,1,0:T(8,128)(2,1)} %copy-done.3) | copy-start | bytes 3145732
  175.0 4.7 %copy-start.6 = (bf16[1,8,8,16,512]{4,3,2,1,0:T(8,128)(2,1)S(1)}, bf16[1,8,8,16,512]{4,3,2,1,0:T(8,128)(2,1)}, u32[]{:S(2)}) copy-start(bf16[1,8,8,16,512]{4,3,2,1,0:T(8,128)(2,1)} %copy-done.5) | copy-start | bytes 3145732
  175.0 4.7 %copy-start.8 = (bf16[1,8,8,16,512]{4,3,2,1,0:T(8,128)(2,1)S(1)}, bf16[1,8,8,16,512]{4,3,2,1,0:T(8,128)(2,1)}, u32[]{:S(2)}) copy-start(bf16[1,8,8,16,512]{4,3,2,1,0:T(8,128)(2,1)} %copy-done.7) | copy-start | bytes 3145732
  175.0 4.7 %copy-start.10 = (bf16[1,8,8,16,512]{4,3,2,1,0:T(8,128)(2,1)S(1)}, bf16[1,8,8,16,512]{4,3,2,1,0:T(8,128)(2,1)}, u32[]{:S(2)}) copy-start(bf16[1,8,8,16,512]{4,3,2,1,0:T(8,128)(2,1)} %copy-done.9) | copy-start | bytes 3145732
  175.0 4.7 %copy-start.14 = (f32[192,1024]{1,0:T(8,128)S(1)}, f32[192,1024]{1,0:T(8,128)}, u32[]{:S(2)}) copy-start(f32[192,1024]{1,0:T(8,128)} %reduce-scatter.2.cloned.1.call-done) | copy-start | bytes 2359300
  175.0 4.7 %copy-start.16 = (f32[192,1024]{1,0:T(8,128)S(1)}, f32[192,1024]{1,0:T(8,128)}, u32[]{:S(2)}) copy-start(f32[192,1024]{1,0:T(8,128)} %copy-done.15) | copy-start | bytes 2359300
  175.0 4.7 %copy-start.17 = (f32[192,1024]{1,0:T(8,128)S(1)}, f32[192,1024]{1,0:T(8,128)}, u32[]{:S(2)}) copy-start(f32[192,1024]{1,0:T(8,128)} %get-tuple-element.15) | copy-start | bytes 2359300
Sparse Core Ops, SparseCore 0:
  94.6 31.3 all-gather.1
  128.9 46.1 reduce-scatter.1

commit v3 on v1

v3 whole, which is shorter than its diff:
```python
import functools

import jax
import jax.numpy as jnp
from jax import lax
from jax.experimental import pallas as pl
from jax.experimental.pallas import tpu as pltpu
from jax.sharding import PartitionSpec as P

MESH = pl.DeviceIdType.MESH
CAP = 8
PAIR = 2 * CAP
BF16 = jnp.bfloat16
F32 = jnp.float32
NT = (((1,), (1,)), ((), ()))
TN = (((0,), (0,)), ((), ()))


def dot(a, b, dims=(((1,), (0,)), ((), ()))):
    return lax.dot_general(a, b, dims, preferred_element_type=F32)


def route_keys(ids, experts, planes):
    per_token, rows = ids.shape
    expert_row = lax.broadcasted_iota(jnp.int32, (experts, rows), 0)
    hits = [ids[k : k + 1, :] == expert_row for k in range(per_token)]
    named = sum(jnp.where(h, 1.0, 0.0) for h in hits).astype(BF16)
    row_at = lax.broadcasted_iota(jnp.int32, (rows, rows), 0)
    col_at = lax.broadcasted_iota(jnp.int32, (rows, rows), 1)
    before = dot(named, jnp.where(row_at < col_at, 1.0, 0.0).astype(BF16))
    ranks = jnp.concatenate(
        [jnp.sum(jnp.where(h, before, 0.0), axis=0, keepdims=True) for h in hits], axis=0
    )
    group = lax.div(ids, jnp.int32(2 * planes))
    local = ids - group * (2 * planes)
    plane = lax.div(local, jnp.int32(2))
    member = group * 2 + (local - plane * 2)
    return plane, member, ranks


def layer_kernel(
    nx, nz,
    ids_hbm, scale_hbm, tok_hbm, grad_hbm, gate_hbm, up_hbm, down_hbm,
    layer_out, gate_out, up_out, down_out,
    ids_v, scale_v, wv, dv,
    zt, zg, zm, xt, xg, slot_t, slot_g,
    pre, hid, hgp, rs_a, rs_b, rs_c, rs_d,
    eo, rx, rz, fin, grads, wout, dout, lout, place_v,
    l_sem, z_send, z_recv, x_send, x_recv, y_send, y_recv, h_send, h_recv,
    s_send, s_recv, e_send, e_recv, f_send, f_recv,
):
    R = nz // 2
    J = 2 * nx
    per_token = ids_v.shape[0]
    Q = zt.shape[3]
    F = hid.shape[2]
    S = J * PAIR
    C = J * CAP
    y = lax.axis_index("dp")
    x = lax.axis_index("grp")
    loc = lax.axis_index("loc")
    z = loc // 2
    core = loc % 2
    me = x * 2 + core
    yp, ym, yo = (y + 1) % 4, (y + 3) % 4, (y + 2) % 4
    y_up, y_down = {"dp": yp}, {"dp": ym}

    def at_plane(p):
        return {"loc": (p % nz) * 2 + core}

    def member_at(j):
        return {"grp": j // 2, "loc": z * 2 + j % 2}

    z_right, z_left = at_plane(z + 1), at_plane(z + nz - 1)

    barrier = pltpu.get_barrier_semaphore()
    greeted = [at_plane(z + d) for d in range(1, nz)] + [y_up, y_down]
    greeted += [member_at((me + o) % J) for o in range(1, J)]
    for device in greeted:
        pl.semaphore_signal(barrier, inc=1, device_id=device, device_id_type=MESH)

    loads = [
        pltpu.make_async_copy(src, dst, l_sem.at[n])
        for n, (src, dst) in enumerate(
            [
                (ids_hbm, ids_v),
                (scale_hbm, scale_v),
                (tok_hbm, zt.at[0, 0]),
                (grad_hbm, zg.at[0, 0]),
                (gate_hbm, wv.at[0]),
                (up_hbm, wv.at[1]),
                (down_hbm, dv),
            ]
        )
    ]
    for load in loads:
        load.start()
    loads[0].wait()
    loads[1].wait()
    plane, member, ranks = route_keys(ids_v[...], nz * J, nz)
    scales = scale_v[...]
    zm[0, 0] = jnp.concatenate(
        [(plane * S + member * PAIR).astype(F32) + ranks, scales], axis=0
    )
    loads[2].wait()
    loads[3].wait()
    pl.semaphore_wait(barrier, len(greeted))

    bufs = (zt, zg, zm)

    def z_copy(kind, way, step, src, dst):
        return pltpu.make_async_remote_copy(
            src_ref=bufs[kind].at[src],
            dst_ref=bufs[kind].at[dst],
            send_sem=z_send.at[way, step, kind],
            recv_sem=z_recv.at[dst[0], dst[1], kind],
            device_id=z_right if way == 0 else z_left,
            device_id_type=MESH,
        )

    def member_copy(src, dst, sems, i, o, j):
        send, recv = sems
        return pltpu.make_async_remote_copy(
            src_ref=src,
            dst_ref=dst,
            send_sem=send.at[i, o],
            recv_sem=recv.at[i, o],
            device_id=member_at(j),
            device_id_type=MESH,
        )

    def exchange(kind):
        return (
            (xt, slot_t.at[y], (x_send.at[0], x_recv.at[0])),
            (xg, slot_g, (x_send.at[1], x_recv.at[1])),
            (eo, rx, (e_send, e_recv)),
        )[kind]

    def exchange_own(kind, i):
        src, dst, sems = exchange(kind)
        return pltpu.make_async_copy(src.at[i, me], dst.at[i, me], sems[1].at[i, 0])

    def exchange_copy(kind, i, o):
        src, dst, sems = exchange(kind)
        j = (me + o) % J
        return member_copy(src.at[i, j], dst.at[i, me], sems, i, o, j)

    def exchange_arrival(kind, i, o):
        src, dst, sems = exchange(kind)
        return member_copy(
            src.at[i, 0], dst.at[i, (me + J - o) % J], sems, i, o, (me + o) % J
        )

    def exchange_start(kind, i):
        exchange_own(kind, i).start()
        for o in range(1, J):
            exchange_copy(kind, i, o).start()

    def exchange_wait(kind, i):
        exchange_own(kind, i).wait()
        for o in range(1, J):
            exchange_arrival(kind, i, o).wait_recv()

    def dp_copy(ref, dst, send, recv, up):
        return pltpu.make_async_remote_copy(
            src_ref=ref,
            dst_ref=dst,
            send_sem=send,
            recv_sem=recv,
            device_id=y_up if up else y_down,
            device_id_type=MESH,
        )

    def gather(kind, k, i, arrival=False):
        buf, half, send, recv = (
            (slot_t, J // 2, y_send, y_recv),
            (hid, F // 2, h_send, h_recv),
        )[kind]
        lower, upper = pl.ds(0, half), pl.ds(half, half)
        if arrival:
            ref = (buf.at[ym, i], buf.at[yp, i], buf.at[yo, i, lower], buf.at[yo, i, upper])[k]
        else:
            ref = (buf.at[y, i], buf.at[y, i], buf.at[ym, i, lower], buf.at[yp, i, upper])[k]
        return dp_copy(ref, ref, send.at[i, k], recv.at[i, k], k % 2 == 0)

    def reduce(k, i):
        half = F // 2
        lower, upper = pl.ds(0, half), pl.ds(half, half)
        src = (hgp.at[i, yo, lower], hgp.at[i, yo, upper], hgp.at[i, yp], hgp.at[i, ym])[k]
        dst = (rs_a, rs_b, rs_c, rs_d)[k].at[i]
        return dp_copy(src, dst, s_send.at[i, k], s_recv.at[i, k], k % 2 == 0)

    def return_copy(h, i):
        return pltpu.make_async_remote_copy(
            src_ref=rz.at[i, h],
            dst_ref=fin.at[i, h],
            send_sem=f_send.at[i, h],
            recv_sem=f_recv.at[i, h],
            device_id=at_plane(z + i) if h == 0 else at_plane(z + nz - i - 1),
            device_id_type=MESH,
        )

    def return_own():
        return pltpu.make_async_copy(rz.at[0, 0], fin.at[0, 0], f_recv.at[0, 0])

    def select(i):
        marks, weights = [], 0.0
        for h in range(2):
            row_key = (
                lax.broadcasted_iota(jnp.int32, (S, zm.shape[3]), 0) + (z * S - h * CAP)
            ).astype(F32)
            table = zm[i, h]
            mark = 0.0
            for k in range(per_token):
                hit = table[k : k + 1, :] == row_key
                mark = mark + jnp.where(hit, 1.0, 0.0)
                weights = weights + jnp.where(hit, table[per_token + k : per_token + k + 1, :], 0.0)
            marks.append(mark)
        place = jnp.concatenate(marks, axis=1).astype(BF16)
        row_scale = jnp.sum(weights, axis=1, keepdims=True)
        xt[i] = dot(place, zt[i].reshape(-1, Q)).astype(BF16).reshape(J, PAIR, Q)
        xg[i] = (dot(place, zg[i].reshape(-1, Q)) * row_scale).astype(BF16).reshape(J, PAIR, Q)

    def z_stage(i):
        @pl.when(i >= 1)
        def _():
            for kind in (0, 2):
                z_copy(kind, 1, 0, (i, 0), (i, 0)).wait_recv()

        @pl.when(i < R - 1)
        def _():
            for kind in (0, 2):
                z_copy(kind, 1, i, (i, 0), (i + 1, 0)).start()

        for kind in (0, 2):
            z_copy(kind, 0, 0, (i, 1), (i, 1)).wait_recv()

        @pl.when(i < R - 1)
        def _():
            for kind in (0, 2):
                z_copy(kind, 0, i + 1, (i, 1), (i + 1, 1)).start()

        @pl.when(i >= 1)
        def _():
            z_copy(1, 1, 0, (i, 0), (i, 0)).wait_recv()

        @pl.when(i < R - 1)
        def _():
            z_copy(1, 1, i, (i, 0), (i + 1, 0)).start()

        @pl.when(i == R - 1)
        def _():
            z_copy(1, 1, R - 1, (R - 1, 0), (R - 1, 1)).start()

        z_copy(1, 0, 0, (i, 1), (i, 1)).wait_recv()

        @pl.when(i < R - 2)
        def _():
            z_copy(1, 0, i + 1, (i, 1), (i + 1, 1)).start()

        select(i)
        exchange_start(0, i)
        exchange_start(1, i)

    def x_stage(i):
        exchange_wait(0, i)
        gather(0, 0, i).start()
        gather(0, 1, i).start()
        exchange_wait(1, i)

    def relay_stage(kind, i):
        for k in range(2):
            gather(kind, k, i, True).wait_recv()
            gather(kind, k + 2, i).start()

    def relay_wait(kind, i):
        gather(kind, 2, i, True).wait_recv()
        gather(kind, 3, i, True).wait_recv()

    def hidden_stage(i):
        relay_wait(0, i)
        rows = jnp.concatenate([slot_t[q, i].reshape(S, Q) for q in range(4)], axis=1)
        both = dot(wv[...].reshape(2 * F, 4 * Q), rows, NT)
        pre[i] = both
        g, u = both[0:F], both[F : 2 * F]
        hid[y, i] = (g * jax.nn.sigmoid(g) * u).astype(BF16)
        gather(1, 0, i).start()
        gather(1, 1, i).start()

    def down_stage(i):
        relay_wait(1, i)
        total = dot(hid[:, i].reshape(4 * F, S), dv[...], TN)
        eo[i] = total.astype(BF16).reshape(J, PAIR, Q)
        exchange_start(2, i)

    def return_stage(i):
        exchange_wait(2, i)
        row = lax.broadcasted_iota(jnp.int32, (S, S), 0)
        col = lax.broadcasted_iota(jnp.int32, (S, S), 1)
        h = lax.div(row, jnp.int32(C))
        j = lax.div(row - h * C, jnp.int32(CAP))
        source = j * PAIR + h * CAP + (row - h * C - j * CAP)
        swap = jnp.where(col == source, 1.0, 0.0).astype(BF16)
        rz[i] = dot(swap, rx[i].reshape(S, Q)).astype(BF16).reshape(2, C, Q)

        @pl.when(i >= 1)
        def _():
            return_copy(0, i).start()

        @pl.when(i == 0)
        def _():
            return_own().start()

        return_copy(1, i).start()

    def sum_first(i):
        part = dot(dv[...], slot_g[i].reshape(S, Q), NT)
        hgp[i] = part.reshape(4, F, S)
        reduce(0, i).start()
        reduce(1, i).start()

    def sum_second(i):
        half = F // 2
        reduce(0, i).wait_recv()
        hgp[i, yp, 0:half] = hgp[i, yp, 0:half] + rs_a[i]
        reduce(2, i).start()
        reduce(1, i).wait_recv()
        hgp[i, ym, half:F] = hgp[i, ym, half:F] + rs_b[i]
        reduce(3, i).start()

    def sum_last(i):
        reduce(2, i).wait_recv()
        reduce(3, i).wait_recv()
        hidden_grad = hgp[i, y] + rs_c[i] + rs_d[i]
        g, u = pre[i, 0:F], pre[i, F : 2 * F]
        s = jax.nn.sigmoid(g)
        gate_grad = hidden_grad * u * s * (1.0 + g * (1.0 - s))
        up_grad = hidden_grad * (g * s)
        grads[i] = jnp.concatenate([gate_grad, up_grad], axis=0).astype(BF16)

    for kind in (0, 2, 1):
        z_copy(kind, 0, 0, (0, 0), (0, 1)).start()

    delta = z - plane
    delta = jnp.where(delta < 0, delta + nz, delta)
    back = jnp.where(delta < R, delta * 2, (nz - 1 - delta) * 2 + 1)
    row_of = (back * C + member * CAP).astype(F32) + ranks
    packed = jnp.concatenate([row_of, scales], axis=0)
    tokens = packed.shape[1]
    packed = jnp.concatenate(
        [packed, jnp.zeros((tokens - 2 * per_token, tokens), F32)], axis=0
    ).T
    for r in range(R):
        lane = (lax.broadcasted_iota(jnp.int32, (tokens, 2 * C), 1) + r * 2 * C).astype(F32)
        weight = 0.0
        for k in range(per_token):
            hit = packed[:, k : k + 1] == lane
            weight = weight + jnp.where(hit, packed[:, per_token + k : per_token + k + 1], 0.0)
        for part in range(3):
            piece = weight.astype(BF16)
            place_v[part, :, r * 2 * C : (r + 1) * 2 * C] = piece
            weight = weight - piece.astype(F32)
    for load in loads[4:]:
        load.wait()

    stages = (
        (0, z_stage),
        (1, x_stage),
        (2, functools.partial(relay_stage, 0)),
        (3, hidden_stage),
        (4, functools.partial(relay_stage, 1)),
        (5, down_stage),
        (6, return_stage),
        (6, sum_first),
        (7, sum_second),
        (8, sum_last),
    )

    def step(i, carry):
        for lag, stage in stages:

            @pl.when((i >= lag) & (i < R + lag))
            def _(lag=lag, stage=stage):
                stage(i - lag)

        return carry

    lax.fori_loop(0, R + 8, step, 0)

    flat_g = slot_g[...].reshape(R * S, Q)
    for q in range(4):
        lhs = jnp.concatenate([hid[q, r] for r in range(R)], axis=1)
        dout[q * F : (q + 1) * F] = dot(lhs, flat_g).astype(BF16)
    stores = [pltpu.make_async_copy(dout, down_out, l_sem.at[0])]
    stores[0].start()
    lhs = jnp.concatenate([grads[r] for r in range(R)], axis=1)
    for q in range(4):
        res = dot(lhs, slot_t[q].reshape(R * S, Q)).astype(BF16)
        wout[0, :, q * Q : (q + 1) * Q] = res[0:F]
        wout[1, :, q * Q : (q + 1) * Q] = res[F : 2 * F]
    stores.append(pltpu.make_async_copy(wout.at[0], gate_out, l_sem.at[1]))
    stores.append(pltpu.make_async_copy(wout.at[1], up_out, l_sem.at[2]))
    stores[1].start()
    stores[2].start()

    def arrivals(i, carry):
        @pl.when(i >= 1)
        def _():
            return_copy(0, i).wait_recv()

        return_copy(1, i).wait_recv()
        return carry

    return_own().wait()
    lax.fori_loop(0, R, arrivals, 0)
    rows = fin[...].reshape(R * S, Q)
    total = dot(place_v[0], rows) + dot(place_v[1], rows) + dot(place_v[2], rows)
    lout[...] = total.astype(BF16)
    stores.append(pltpu.make_async_copy(lout, layer_out, l_sem.at[3]))
    stores[3].start()

    def drain(i, carry):
        for kind in (0, 2):
            z_copy(kind, 0, i, (0, 0), (0, 1)).wait_send()

        @pl.when(i < R - 1)
        def _():
            z_copy(1, 0, i, (0, 0), (0, 1)).wait_send()
            for kind in (0, 2):
                z_copy(kind, 1, i, (0, 0), (0, 1)).wait_send()

        z_copy(1, 1, i, (0, 0), (0, 1)).wait_send()
        for kind in range(3):
            for o in range(1, J):
                exchange_copy(kind, i, o).wait_send()
        for k in range(4):
            gather(0, k, i).wait_send()
            gather(1, k, i).wait_send()
            reduce(k, i).wait_send()

        @pl.when(i >= 1)
        def _():
            return_copy(0, i).wait_send()

        return_copy(1, i).wait_send()
        return carry

    lax.fori_loop(0, R, drain, 0)
    for store in stores:
        store.wait()


def body(tokens, grad_out, expert_ids, gate_scale, gate_weight, up_weight, down_weight):
    nx = lax.axis_size("grp")
    nz = lax.axis_size("loc") // 2
    rows, Q = tokens.shape
    per_token = expert_ids.shape[1]
    F = gate_weight.shape[1]
    R, J = nz // 2, 2 * nx
    S, C = J * PAIR, J * CAP
    hbm = pl.BlockSpec(memory_space=pl.ANY)
    dma = pltpu.SemaphoreType.DMA
    outs = pl.pallas_call(
        functools.partial(layer_kernel, nx, nz),
        out_shape=(
            jax.ShapeDtypeStruct((rows, Q), BF16),
            jax.ShapeDtypeStruct((F, 4 * Q), BF16),
            jax.ShapeDtypeStruct((F, 4 * Q), BF16),
            jax.ShapeDtypeStruct((4 * F, Q), BF16),
        ),
        in_specs=[hbm] * 7,
        out_specs=(hbm,) * 4,
        scratch_shapes=[
            pltpu.VMEM((per_token, rows), jnp.int32),
            pltpu.VMEM((per_token, rows), F32),
            pltpu.VMEM((2, F, 4 * Q), BF16),
            pltpu.VMEM((4 * F, Q), BF16),
            pltpu.VMEM((R, 2, rows, Q), BF16),
            pltpu.VMEM((R, 2, rows, Q), BF16),
            pltpu.VMEM((R, 2, 2 * per_token, rows), F32),
            pltpu.VMEM((R, J, PAIR, Q), BF16),
            pltpu.VMEM((R, J, PAIR, Q), BF16),
            pltpu.VMEM((4, R, J, PAIR, Q), BF16),
            pltpu.VMEM((R, J, PAIR, Q), BF16),
            pltpu.VMEM((R, 2 * F, S), F32),
            pltpu.VMEM((4, R, F, S), BF16),
            pltpu.VMEM((R, 4, F, S), F32),
            pltpu.VMEM((R, F // 2, S), F32),
            pltpu.VMEM((R, F // 2, S), F32),
            pltpu.VMEM((R, F, S), F32),
            pltpu.VMEM((R, F, S), F32),
            pltpu.VMEM((R, J, PAIR, Q), BF16),
            pltpu.VMEM((R, J, PAIR, Q), BF16),
            pltpu.VMEM((R, 2, C, Q), BF16),
            pltpu.VMEM((R, 2, C, Q), BF16),
            pltpu.VMEM((R, 2 * F, S), BF16),
            pltpu.VMEM((2, F, 4 * Q), BF16),
            pltpu.VMEM((4 * F, Q), BF16),
            pltpu.VMEM((rows, Q), BF16),
            pltpu.VMEM((3, rows, R * S), BF16),
            dma((7,)),
            dma((2, R, 3)),
            dma((R, 2, 3)),
            dma((2, R, J)),
            dma((2, R, J)),
            dma((R, 4)),
            dma((R, 4)),
            dma((R, 4)),
            dma((R, 4)),
            dma((R, 4)),
            dma((R, 4)),
            dma((R, J)),
            dma((R, J)),
            dma((R, 2)),
            dma((R, 2)),
        ],
        compiler_params=pltpu.CompilerParams(
            collective_id=0, has_side_effects=True, vmem_limit_bytes=56 * 1024 * 1024
        ),
    )(
        expert_ids.T,
        gate_scale.T,
        tokens,
        grad_out,
        gate_weight[0],
        up_weight[0],
        down_weight[0],
    )
    return (outs[0], outs[1][None], outs[2][None], outs[3][None])


def solution(mesh):
    return jax.shard_map(
        body,
        mesh=mesh,
        in_specs=(
            P(("grp", "loc"), "dp"),
            P(("grp", "loc"), "dp"),
            P(("grp", "loc"), None),
            P(("grp", "loc"), None),
            P(("grp", "loc"), "dp", None),
            P(("grp", "loc"), "dp", None),
            P(("grp", "loc"), None, "dp"),
        ),
        out_specs=(
            P(("grp", "loc"), "dp"),
            P(("grp", "loc"), "dp", None),
            P(("grp", "loc"), "dp", None),
            P(("grp", "loc"), None, "dp"),
        ),
        check_vma=False,
    )
```

time: 316 us -> 149 us (0.47)
  Pallas kernels: 0 us -> 142 us
  waiting for transfers between devices: 128 us -> 0 us
  blocking collectives: 120 us -> 0 us
  matrix products: 23.1 us -> 0 us
  starting transfers between devices: 16.9 us -> 0 us
  between operations: 14 us -> 0.64 us
  local copies, waits for them, and re-layouts: 11.7 us -> 6.03 us
    pallas_call x0 -> x1, Pallas kernels: none -> 142 us  [body(): pl.pallas_call(functools.partial(layer_kernel, nx, nz), out_shape=(jax.Sh...]
    all_to_all x1 -> x0, blocking collectives: 120 us -> none  [send_rows(): lax.all_to_all(outgoing, ('grp', 'loc'), split_axis=0, concat_axis=0, til...]
    all_gather x2 -> x0, waiting for transfers between devices: 81.7 us -> none  [the longest x1 49.7 us: body(): flat_tokens = lax.all_gather(arrived[:, :quarter], 'dp', axis=1, tiled=True)]
    reduce_scatter x1 -> x0, waiting for transfers between devices: 28.8 us -> none  [body(): lax.psum_scatter(lax.dot_general(down_rows, flat_grads, feature_contract,...]
    dot_general x9 -> x0, matrix products: 23.1 us -> none  [the longest x1 4.5 us: body(): jnp.dot(up_grad, flat_tokens, preferred_element_type=jnp.float32)]
    all_to_all x1 -> x0, waiting for transfers between devices: 17 us -> none  [return_rows(): lax.all_to_all(results, ('grp', 'loc'), split_axis=0, concat_axis=0, tile...]
    all_to_all x1 -> x0, starting transfers between devices: 16.7 us -> none  [return_rows(): lax.all_to_all(results, ('grp', 'loc'), split_axis=0, concat_axis=0, tile...]
    unnamed x30 -> x8, local copies, waits for them, and re-layouts: 2.45 us -> 6.03 us
  transfers between devices with their start and end apart: 4 -> 0, of which waited for: 4 -> 0; matrix products, arithmetic and copies ran while one was open for 5% -> 0% of each run, Pallas kernels for 0% -> 0%
where the time goes in v3:
time: 149 us
  Pallas kernels  142 us (95%)
  local copies, waits for them, and re-layouts  6.03 us (4%)
    pallas_call x1, Pallas kernels, body(): pl.pallas_call(functools.partial(layer_kernel, nx, nz), out_shape=(jax.Sh...  142 us
    unnamed x8, local copies, waits for them, and re-layouts  6.03 us

profile of v3, /device:TPU:1, one launch (start us, length us, event | category | flops | bytes accessed | tf_op | source)
XLA Modules:
  0.0 148.7 jit_solution(2787358232893319659)
XLA Ops:
  0.6 142.0 %shard_map.102 = (bf16[128,512]{1,0:T(8,128)(2,1)}, bf16[192,2048]{1,0:T(8,128)(2,1)}, bf16[192,2048]{1,0:T(8,128)(2,1)}, bf16[768,512]{1,0:T(8,128)(2,1)}) custom-call(s32[4,128]{1,0:T(4,128)} %bitcast.14, f32[4,128]{1,0:T(4,128)} %bitcast.15, bf16[128,512]{1,0:T(8,128)(2,1)} %tok_hbm.1, bf16[128,512]{1,0:T(8,128)(2,1)} %grad_hbm.1, ...), custom_call_target="tpu_custom_call" | custom-call | tf_op jit(solution)/shard_map/pallas_call | solution.py:463
  142.6 1.6 %copy.15 = bf16[128,512]{1,0:T(8,128)(2,1)} copy(bf16[128,512]{1,0:T(8,128)(2,1)} %get-tuple-element.16) | data formatting | bytes 262144
  144.2 0.0 copy-start.1
  144.2 2.2 %copy.16 = bf16[1,192,2048]{2,1,0:T(8,128)(2,1)} copy(bf16[1,192,2048]{2,1,0:T(8,128)(2,1)} %bitcast.10) | data formatting | bytes 1572864
  146.4 0.0 copy-done.1
  146.4 0.0 copy-start
  146.4 0.9 copy.17
  147.3 0.5 copy-done
  147.8 0.9 copy.18
Async XLA Ops:
  144.2 2.2 %copy-start.1 = (bf16[192,2048]{1,0:T(8,128)(2,1)S(1)}, bf16[192,2048]{1,0:T(8,128)(2,1)}, u32[]{:S(2)}) copy-start(bf16[192,2048]{1,0:T(8,128)(2,1)} %get-tuple-element.10) | copy-start | bytes 2359300
  146.4 1.4 copy-start

commit v4 on v3

v4 whole, which is shorter than its diff:
```python
import functools

import jax
import jax.numpy as jnp
from jax import lax
from jax.experimental import pallas as pl
from jax.experimental.pallas import tpu as pltpu
from jax.sharding import PartitionSpec as P

MESH = pl.DeviceIdType.MESH
CAP = 8
PAIR = 2 * CAP
BF16 = jnp.bfloat16
F32 = jnp.float32
NT = (((1,), (1,)), ((), ()))
TN = (((0,), (0,)), ((), ()))


def dot(a, b, dims=(((1,), (0,)), ((), ()))):
    return lax.dot_general(a, b, dims, preferred_element_type=F32)


def route_keys(ids, experts, planes):
    per_token, rows = ids.shape
    expert_row = lax.broadcasted_iota(jnp.int32, (experts, rows), 0)
    hits = [ids[k : k + 1, :] == expert_row for k in range(per_token)]
    named = sum(jnp.where(h, 1.0, 0.0) for h in hits).astype(BF16)
    row_at = lax.broadcasted_iota(jnp.int32, (rows, rows), 0)
    col_at = lax.broadcasted_iota(jnp.int32, (rows, rows), 1)
    before = dot(named, jnp.where(row_at < col_at, 1.0, 0.0).astype(BF16))
    ranks = jnp.concatenate(
        [jnp.sum(jnp.where(h, before, 0.0), axis=0, keepdims=True) for h in hits], axis=0
    )
    group = lax.div(ids, jnp.int32(2 * planes))
    local = ids - group * (2 * planes)
    plane = lax.div(local, jnp.int32(2))
    member = group * 2 + (local - plane * 2)
    return plane, member, ranks


def layer_kernel(
    nx, nz,
    ids_hbm, scale_hbm, tok_hbm, grad_hbm, gate_hbm, up_hbm, down_hbm,
    layer_out, gate_out, up_out, down_out,
    ids_v, scale_v, wv, dv,
    zt, zg, zm, xs, sx, slot_t,
    pre, hid, hgp, hgs, rs_half, rs_full,
    eo, rx, rz, fin, grads, place_v,
    far, l_sem, z_send, z_recv, x_send, x_recv, y_send, y_recv, s_send, s_recv, f_send, f_recv,
    far_send, far_recv,
):
    R = nz // 2
    J = 2 * nx
    per_token = ids_v.shape[0]
    Q = zt.shape[3]
    F = hid.shape[2]
    S = J * PAIR
    C = J * CAP
    y = lax.axis_index("dp")
    x = lax.axis_index("grp")
    loc = lax.axis_index("loc")
    z = loc // 2
    core = loc % 2
    me = x * 2 + core
    yp, ym, yo = (y + 1) % 4, (y + 3) % 4, (y + 2) % 4
    y_up, y_down = {"dp": yp}, {"dp": ym}

    def at_plane(p):
        return {"loc": (p % nz) * 2 + core}

    def member_at(j):
        return {"grp": j // 2, "loc": z * 2 + j % 2}

    z_right, z_left = at_plane(z + 1), at_plane(z + nz - 1)

    barrier = pltpu.get_barrier_semaphore()
    greeted = [at_plane(z + d) for d in range(1, nz)] + [y_up, y_down]
    greeted += [member_at((me + o) % J) for o in range(1, J)]
    for device in greeted:
        pl.semaphore_signal(barrier, inc=1, device_id=device, device_id_type=MESH)

    loads = [
        pltpu.make_async_copy(src, dst, l_sem.at[n])
        for n, (src, dst) in enumerate(
            [
                (ids_hbm, ids_v),
                (scale_hbm, scale_v),
                (tok_hbm, zt.at[0, 0]),
                (grad_hbm, zg.at[0, 0]),
                (gate_hbm, wv.at[0]),
                (up_hbm, wv.at[1]),
                (down_hbm, dv),
            ]
        )
    ]
    for load in loads:
        load.start()
    loads[0].wait()
    loads[1].wait()
    plane, member, ranks = route_keys(ids_v[...], nz * J, nz)
    scales = scale_v[...]
    zm[0, 0] = jnp.concatenate(
        [(plane * S + member * PAIR).astype(F32) + ranks, scales], axis=0
    )
    loads[2].wait()
    loads[3].wait()
    pl.semaphore_wait(barrier, len(greeted))

    bufs = (zt, zg, zm)

    def z_copy(kind, way, src, dst):
        return pltpu.make_async_remote_copy(
            src_ref=bufs[kind].at[src],
            dst_ref=bufs[kind].at[dst],
            send_sem=z_send.at[way, kind],
            recv_sem=z_recv.at[dst[0], dst[1], kind],
            device_id=z_right if way == 0 else z_left,
            device_id_type=MESH,
        )

    def exchange(kind):
        return ((xs, sx), (eo, rx))[kind]

    def exchange_start(kind, i):
        src, dst = exchange(kind)
        pltpu.make_async_copy(src.at[i, me], dst.at[i, me], x_recv.at[kind, i]).start()
        for o in range(1, J):
            j = (me + o) % J
            pltpu.make_async_remote_copy(
                src_ref=src.at[i, j],
                dst_ref=dst.at[i, me],
                send_sem=x_send.at[kind],
                recv_sem=x_recv.at[kind, i],
                device_id=member_at(j),
                device_id_type=MESH,
            ).start()

    def exchange_wait(kind, i):
        src, dst = exchange(kind)
        pltpu.make_async_copy(src.at[i], dst.at[i], x_recv.at[kind, i]).wait()

    def dp_copy(ref, dst, send, recv, up):
        return pltpu.make_async_remote_copy(
            src_ref=ref,
            dst_ref=dst,
            send_sem=send,
            recv_sem=recv,
            device_id=y_up if up else y_down,
            device_id_type=MESH,
        )

    def gather_buffer(kind):
        return (slot_t, hid)[kind]

    def gather(kind, k, i):
        buf = gather_buffer(kind)
        half = buf.shape[2] // 2
        lower, upper = pl.ds(0, half), pl.ds(half, half)
        ref = (buf.at[y, i], buf.at[y, i], buf.at[ym, i, lower], buf.at[yp, i, upper])[k]
        return dp_copy(ref, ref, y_send.at[kind], y_recv.at[kind, k // 2, i], k % 2 == 0)

    def reduce(k, i):
        half = F // 2
        lower, upper = pl.ds(0, half), pl.ds(half, half)
        src = (hgs.at[i, 0, lower], hgs.at[i, 0, upper], hgs.at[i, 1], hgs.at[i, 2])[k]
        dst = (rs_half, rs_full)[k // 2].at[i, k % 2]
        return dp_copy(src, dst, s_send, s_recv.at[k // 2, i], k % 2 == 0)

    def arrived(ref, sem):
        pltpu.make_async_copy(ref, ref, sem).wait()

    def return_copy(h, i):
        return pltpu.make_async_remote_copy(
            src_ref=rz.at[2 * i + h],
            dst_ref=fin.at[2 * i + h],
            send_sem=f_send,
            recv_sem=f_recv,
            device_id=at_plane(z + i) if h == 0 else at_plane(z + nz - i - 1),
            device_id_type=MESH,
        )

    def far_copy(way, leg):
        part = pl.ds(way * (C // 2), C // 2)
        last = 2 * R - 1
        return pltpu.make_async_remote_copy(
            src_ref=rz.at[last, part] if leg == 0 else far.at[way],
            dst_ref=far.at[way] if leg == 0 else fin.at[last, part],
            send_sem=f_send if leg == 0 else far_send,
            recv_sem=far_recv.at[way] if leg == 0 else f_recv,
            device_id=at_plane(z + R // 2) if way == 0 else at_plane(z + nz - R // 2),
            device_id_type=MESH,
        )

    def far_stage(i):
        for way in range(2):
            arrived(far.at[way], far_recv.at[way])
            far_copy(way, 1).start()

    def return_own():
        return pltpu.make_async_copy(rz.at[0], fin.at[0], f_recv)

    def select(i):
        marks, weights = [], 0.0
        for h in range(2):
            row_key = (
                lax.broadcasted_iota(jnp.int32, (S, zm.shape[3]), 0) + (z * S - h * CAP)
            ).astype(F32)
            table = zm[i, h]
            mark = 0.0
            for k in range(per_token):
                hit = table[k : k + 1, :] == row_key
                mark = mark + jnp.where(hit, 1.0, 0.0)
                weights = weights + jnp.where(hit, table[per_token + k : per_token + k + 1, :], 0.0)
            marks.append(mark)
        place = jnp.concatenate(marks, axis=1).astype(BF16)
        row_scale = jnp.sum(weights, axis=1, keepdims=True)
        picked_t = dot(place, zt[i].reshape(-1, Q)).astype(BF16)
        picked_g = (dot(place, zg[i].reshape(-1, Q)) * row_scale).astype(BF16)
        xs[i, :, :, 0:Q] = picked_t.reshape(J, PAIR, Q)
        xs[i, :, :, Q : 2 * Q] = picked_g.reshape(J, PAIR, Q)

    def z_stage(i):
        @pl.when(i >= 1)
        def _():
            for kind in (0, 2):
                z_copy(kind, 1, (i, 0), (i, 0)).wait_recv()

        @pl.when(i < R - 1)
        def _():
            for kind in (0, 2):
                z_copy(kind, 1, (i, 0), (i + 1, 0)).start()

        for kind in (0, 2):
            z_copy(kind, 0, (i, 1), (i, 1)).wait_recv()

        @pl.when(i < R - 1)
        def _():
            for kind in (0, 2):
                z_copy(kind, 0, (i, 1), (i + 1, 1)).start()

        @pl.when(i >= 1)
        def _():
            z_copy(1, 1, (i, 0), (i, 0)).wait_recv()

        @pl.when(i < R - 1)
        def _():
            z_copy(1, 1, (i, 0), (i + 1, 0)).start()

        @pl.when(i == R - 1)
        def _():
            z_copy(1, 1, (R - 1, 0), (R - 1, 1)).start()

        z_copy(1, 0, (i, 1), (i, 1)).wait_recv()

        @pl.when(i < R - 2)
        def _():
            z_copy(1, 0, (i, 1), (i + 1, 1)).start()

    def select_stage(i):
        select(i)
        exchange_start(0, i)

    def x_stage(i):
        exchange_wait(0, i)
        slot_t[y, i] = sx[i, :, :, 0:Q]
        gather(0, 0, i).start()
        gather(0, 1, i).start()

    def relay_stage(kind, i):
        buf = gather_buffer(kind)
        arrived(buf.at[pl.ds(0, 2), i], y_recv.at[kind, 0, i])
        gather(kind, 2, i).start()
        gather(kind, 3, i).start()

    def relay_wait(kind, i):
        arrived(gather_buffer(kind).at[yo, i], y_recv.at[kind, 1, i])

    def hidden_stage(i):
        relay_wait(0, i)
        rows = jnp.concatenate([slot_t[q, i].reshape(S, Q) for q in range(4)], axis=1)
        both = dot(wv[...].reshape(2 * F, 4 * Q), rows, NT)
        pre[i] = both
        g, u = both[0:F], both[F : 2 * F]
        hid[y, i] = (g * jax.nn.sigmoid(g) * u).astype(BF16)
        gather(1, 0, i).start()
        gather(1, 1, i).start()

    def down_stage(i):
        relay_wait(1, i)
        total = dot(hid[:, i].reshape(4 * F, S), dv[...], TN)
        eo[i] = total.astype(BF16).reshape(J, PAIR, Q)
        exchange_start(1, i)

    def return_stage(i):
        exchange_wait(1, i)
        row = lax.broadcasted_iota(jnp.int32, (S, S), 0)
        col = lax.broadcasted_iota(jnp.int32, (S, S), 1)
        h = lax.div(row, jnp.int32(C))
        j = lax.div(row - h * C, jnp.int32(CAP))
        source = j * PAIR + h * CAP + (row - h * C - j * CAP)
        swap = jnp.where(col == source, 1.0, 0.0).astype(BF16)
        rz[pl.ds(2 * i, 2)] = dot(swap, rx[i].reshape(S, Q)).astype(BF16).reshape(2, C, Q)

        @pl.when(i >= 1)
        def _():
            return_copy(0, i).start()

        @pl.when(i == 0)
        def _():
            return_own().start()

        @pl.when(i < R - 1)
        def _():
            return_copy(1, i).start()

        @pl.when(i == R - 1)
        def _():
            far_copy(0, 0).start()
            far_copy(1, 0).start()

    def sum_first(i):
        part = dot(dv[...], sx[i, :, :, Q : 2 * Q].reshape(S, Q), NT)
        hgp[i] = part.reshape(4, F, S)
        hgs[i, 0] = hgp[i, yo].astype(BF16)
        reduce(0, i).start()
        reduce(1, i).start()

    def sum_second(i):
        half = F // 2
        arrived(rs_half.at[i], s_recv.at[0, i])
        hgs[i, 1, 0:half] = (hgp[i, yp, 0:half] + rs_half[i, 0].astype(F32)).astype(BF16)
        hgs[i, 1, half:F] = hgp[i, yp, half:F].astype(BF16)
        reduce(2, i).start()
        hgs[i, 2, half:F] = (hgp[i, ym, half:F] + rs_half[i, 1].astype(F32)).astype(BF16)
        hgs[i, 2, 0:half] = hgp[i, ym, 0:half].astype(BF16)
        reduce(3, i).start()

    def sum_last(i):
        arrived(rs_full.at[i], s_recv.at[1, i])
        hidden_grad = hgp[i, y] + rs_full[i, 0].astype(F32) + rs_full[i, 1].astype(F32)
        g, u = pre[i, 0:F], pre[i, F : 2 * F]
        s = jax.nn.sigmoid(g)
        gate_grad = hidden_grad * u * s * (1.0 + g * (1.0 - s))
        up_grad = hidden_grad * (g * s)
        grads[i] = jnp.concatenate([gate_grad, up_grad], axis=0).astype(BF16)

    for kind in (0, 2, 1):
        z_copy(kind, 0, (0, 0), (0, 1)).start()

    delta = z - plane
    delta = jnp.where(delta < 0, delta + nz, delta)
    back = jnp.where(delta < R, delta * 2, (nz - 1 - delta) * 2 + 1)
    row_of = (back * C + member * CAP).astype(F32) + ranks
    packed = jnp.concatenate([row_of, scales], axis=0)
    tokens = packed.shape[1]
    packed = jnp.concatenate(
        [packed, jnp.zeros((tokens - 2 * per_token, tokens), F32)], axis=0
    ).T
    for r in range(R):
        lane = (lax.broadcasted_iota(jnp.int32, (tokens, 2 * C), 1) + r * 2 * C).astype(F32)
        weight = 0.0
        for k in range(per_token):
            hit = packed[:, k : k + 1] == lane
            weight = weight + jnp.where(hit, packed[:, per_token + k : per_token + k + 1], 0.0)
        for part in range(3):
            piece = weight.astype(BF16)
            place_v[part, :, r * 2 * C : (r + 1) * 2 * C] = piece
            weight = weight - piece.astype(F32)
    for load in loads[4:]:
        load.wait()

    stages = (
        (0, z_stage),
        (6, return_stage),
        (5, down_stage),
        (4, functools.partial(relay_stage, 1)),
        (3, hidden_stage),
        (2, functools.partial(relay_stage, 0)),
        (1, x_stage),
        (0, select_stage),
    )
    sums = ((10, sum_last), (9, sum_second), (8, sum_first))

    def step(i, carry):
        for lag, stage in stages:

            @pl.when((i >= lag) & (i < R + lag))
            def _(lag=lag, stage=stage):
                stage(i - lag)

        @pl.when(i == R + 6)
        def _():
            far_stage(i)

        for lag, stage in sums:

            @pl.when((i >= lag) & (i < R // 2 + lag))
            def _(lag=lag, stage=stage):
                stage((i - lag) * 2)
                stage((i - lag) * 2 + 1)

        return carry

    lax.fori_loop(0, R + 7, step, 0)

    flat_g = sx[:, :, :, Q : 2 * Q].reshape(R * S, Q)
    for q in range(4):
        lhs = jnp.concatenate([hid[q, r] for r in range(R)], axis=1)
        down_out[q * F : (q + 1) * F] = dot(lhs, flat_g).astype(BF16)
    lhs = jnp.concatenate([grads[r] for r in range(R)], axis=1)
    for q in range(4):
        res = dot(lhs, slot_t[q].reshape(R * S, Q)).astype(BF16)
        gate_out[:, q * Q : (q + 1) * Q] = res[0:F]
        up_out[:, q * Q : (q + 1) * Q] = res[F : 2 * F]

    arrived(zt.at[:, 0], z_send.at[0, 0])
    arrived(zm.at[:, 0], z_send.at[0, 2])
    arrived(zg.at[pl.ds(0, R - 1), 0], z_send.at[0, 1])
    arrived(zt.at[pl.ds(0, R - 1), 0], z_send.at[1, 0])
    arrived(zm.at[pl.ds(0, R - 1), 0], z_send.at[1, 2])
    arrived(zg.at[:, 0], z_send.at[1, 1])
    arrived(xs.at[:, pl.ds(0, J - 1)], x_send.at[0])
    arrived(eo.at[:, pl.ds(0, J - 1)], x_send.at[1])
    arrived(slot_t.at[pl.ds(0, 3)], y_send.at[0])
    arrived(hid.at[pl.ds(0, 3)], y_send.at[1])
    arrived(hgs, s_send)
    arrived(fin, f_recv)
    rows = fin[...].reshape(R * S, Q)
    total = dot(place_v[0], rows) + dot(place_v[1], rows) + dot(place_v[2], rows)
    layer_out[...] = total.astype(BF16)
    arrived(rz.at[pl.ds(0, 2 * R - 1)], f_send)
    arrived(far, far_send)


def body(tokens, grad_out, expert_ids, gate_scale, gate_weight, up_weight, down_weight):
    nx = lax.axis_size("grp")
    nz = lax.axis_size("loc") // 2
    rows, Q = tokens.shape
    per_token = expert_ids.shape[1]
    F = gate_weight.shape[1]
    R, J = nz // 2, 2 * nx
    S, C = J * PAIR, J * CAP
    hbm = pl.BlockSpec(memory_space=pltpu.HBM)
    dma = pltpu.SemaphoreType.DMA
    outs = pl.pallas_call(
        functools.partial(layer_kernel, nx, nz),
        out_shape=(
            jax.ShapeDtypeStruct((rows, Q), BF16),
            jax.ShapeDtypeStruct((F, 4 * Q), BF16),
            jax.ShapeDtypeStruct((F, 4 * Q), BF16),
            jax.ShapeDtypeStruct((4 * F, Q), BF16),
        ),
        in_specs=[hbm] * 7,
        out_specs=(pl.BlockSpec(memory_space=pltpu.VMEM),) * 4,
        scratch_shapes=[
            pltpu.VMEM((per_token, rows), jnp.int32),
            pltpu.VMEM((per_token, rows), F32),
            pltpu.VMEM((2, F, 4 * Q), BF16),
            pltpu.VMEM((4 * F, Q), BF16),
            pltpu.VMEM((R, 2, rows, Q), BF16),
            pltpu.VMEM((R, 2, rows, Q), BF16),
            pltpu.VMEM((R, 2, 2 * per_token, rows), F32),
            pltpu.VMEM((R, J, PAIR, 2 * Q), BF16),
            pltpu.VMEM((R, J, PAIR, 2 * Q), BF16),
            pltpu.VMEM((4, R, J, PAIR, Q), BF16),
            pltpu.VMEM((R, 2 * F, S), F32),
            pltpu.VMEM((4, R, F, S), BF16),
            pltpu.VMEM((R, 4, F, S), F32),
            pltpu.VMEM((R, 3, F, S), BF16),
            pltpu.VMEM((R, 2, F // 2, S), BF16),
            pltpu.VMEM((R, 2, F, S), BF16),
            pltpu.VMEM((R, J, PAIR, Q), BF16),
            pltpu.VMEM((R, J, PAIR, Q), BF16),
            pltpu.VMEM((2 * R, C, Q), BF16),
            pltpu.VMEM((2 * R, C, Q), BF16),
            pltpu.VMEM((R, 2 * F, S), BF16),
            pltpu.VMEM((3, rows, R * S), BF16),
            pltpu.VMEM((2, C // 2, Q), BF16),
            dma((7,)),
            dma((2, 3)),
            dma((R, 2, 3)),
            dma((2,)),
            dma((2, R)),
            dma((2,)),
            dma((2, 2, R)),
            dma(()),
            dma((2, R)),
            dma(()),
            dma(()),
            dma(()),
            dma((2,)),
        ],
        compiler_params=pltpu.CompilerParams(
            collective_id=0, has_side_effects=True, vmem_limit_bytes=48 * 1024 * 1024
        ),
    )(
        *(
            pltpu.with_memory_space_constraint(a, pltpu.HBM)
            for a in (
                expert_ids.T,
                gate_scale.T,
                tokens,
                grad_out,
                gate_weight[0],
                up_weight[0],
                down_weight[0],
            )
        )
    )
    return (outs[0], outs[1][None], outs[2][None], outs[3][None])


def solution(mesh):
    return jax.shard_map(
        body,
        mesh=mesh,
        in_specs=(
            P(("grp", "loc"), "dp"),
            P(("grp", "loc"), "dp"),
            P(("grp", "loc"), None),
            P(("grp", "loc"), None),
            P(("grp", "loc"), "dp", None),
            P(("grp", "loc"), "dp", None),
            P(("grp", "loc"), None, "dp"),
        ),
        out_specs=(
            P(("grp", "loc"), "dp"),
            P(("grp", "loc"), "dp", None),
            P(("grp", "loc"), "dp", None),
            P(("grp", "loc"), None, "dp"),
        ),
        check_vma=False,
    )
```

time: 149 us -> 133 us (0.89)
  Pallas kernels: 142 us -> 128 us
  local copies, waits for them, and re-layouts: 6.03 us -> 3.29 us
    pallas_call x1, Pallas kernels: 142 us -> 128 us  [body(): pl.pallas_call(functools.partial(layer_kernel, nx, nz), out_shape=(jax.Sh...]
    unnamed x8 -> x4, local copies, waits for them, and re-layouts: 6.03 us -> 3.29 us
where the time goes in v4:
time: 133 us; the launch traced here: 132 us
  Pallas kernels  128 us (96%)
  local copies, waits for them, and re-layouts  3.29 us (2%)
    pallas_call x1, Pallas kernels, body(): pl.pallas_call(functools.partial(layer_kernel, nx, nz), out_shape=(jax.Sh...  128 us
    unnamed x4, local copies, waits for them, and re-layouts  3.29 us

profile of v4, /device:TPU:1, one launch (start us, length us, event | category | flops | bytes accessed | tf_op | source)
XLA Modules:
  0.0 132.4 jit_solution(1510105820128168854)
XLA Ops:
  0.6 128.4 %shard_map.102 = (bf16[128,512]{1,0:T(8,128)(2,1)S(1)}, bf16[192,2048]{1,0:T(8,128)(2,1)S(1)}, bf16[192,2048]{1,0:T(8,128)(2,1)S(1)}, bf16[768,512]{1,0:T(8,128)(2,1)S(1)}) custom-call(s32[4,128]{1,0:T(4,128)} %bitcast.14, f32[4,128]{1,0:T(4,128)} %bitcast.15, bf16[128,512]{1,0:T(8,128)(2,1)} %tok_hbm.1, bf16[128,512]{1,0:T(8,128)(2,1)} %grad_hbm.1, ...), custom_call_target="tpu_custom_call" | custom-call | tf_op jit(solution)/shard_map/pallas_call | solution.py:445
  129.1 0.7 copy.15
  129.7 0.9 copy.16
  130.6 0.9 copy.17
  131.5 0.9 copy.18

commit v5 on v4

--- a/solution.py
+++ b/solution.py
@@ -46,8 +46,7 @@
     zt, zg, zm, xs, sx, slot_t,
     pre, hid, hgp, hgs, rs_half, rs_full,
     eo, rx, rz, fin, grads, place_v,
-    far, l_sem, z_send, z_recv, x_send, x_recv, y_send, y_recv, s_send, s_recv, f_send, f_recv,
-    far_send, far_recv,
+    l_sem, z_send, z_recv, x_send, x_recv, y_send, y_recv, s_send, s_recv, f_send, f_recv,
 ):
     R = nz // 2
     J = 2 * nx
@@ -179,23 +178,6 @@
             device_id_type=MESH,
         )
 
-    def far_copy(way, leg):
-        part = pl.ds(way * (C // 2), C // 2)
-        last = 2 * R - 1
-        return pltpu.make_async_remote_copy(
-            src_ref=rz.at[last, part] if leg == 0 else far.at[way],
-            dst_ref=far.at[way] if leg == 0 else fin.at[last, part],
-            send_sem=f_send if leg == 0 else far_send,
-            recv_sem=far_recv.at[way] if leg == 0 else f_recv,
-            device_id=at_plane(z + R // 2) if way == 0 else at_plane(z + nz - R // 2),
-            device_id_type=MESH,
-        )
-
-    def far_stage(i):
-        for way in range(2):
-            arrived(far.at[way], far_recv.at[way])
-            far_copy(way, 1).start()
-
     def return_own():
         return pltpu.make_async_copy(rz.at[0], fin.at[0], f_recv)
 
@@ -309,19 +291,14 @@
         def _():
             return_own().start()
 
-        @pl.when(i < R - 1)
-        def _():
-            return_copy(1, i).start()
-
-        @pl.when(i == R - 1)
-        def _():
-            far_copy(0, 0).start()
-            far_copy(1, 0).start()
-
-    def sum_first(i):
+        return_copy(1, i).start()
+
+    def sum_part(i):
         part = dot(dv[...], sx[i, :, :, Q : 2 * Q].reshape(S, Q), NT)
         hgp[i] = part.reshape(4, F, S)
         hgs[i, 0] = hgp[i, yo].astype(BF16)
+
+    def sum_first(i):
         reduce(0, i).start()
         reduce(1, i).start()
 
@@ -378,6 +355,7 @@
         (2, functools.partial(relay_stage, 0)),
         (1, x_stage),
         (0, select_stage),
+        (2, sum_part),
     )
     sums = ((10, sum_last), (9, sum_second), (8, sum_first))
 
@@ -387,10 +365,6 @@
             @pl.when((i >= lag) & (i < R + lag))
             def _(lag=lag, stage=stage):
                 stage(i - lag)
-
-        @pl.when(i == R + 6)
-        def _():
-            far_stage(i)
 
         for lag, stage in sums:
 
@@ -401,7 +375,7 @@
 
         return carry
 
-    lax.fori_loop(0, R + 7, step, 0)
+    lax.fori_loop(0, R + 6, step, 0)
 
     flat_g = sx[:, :, :, Q : 2 * Q].reshape(R * S, Q)
     for q in range(4):
@@ -429,7 +403,15 @@
     total = dot(place_v[0], rows) + dot(place_v[1], rows) + dot(place_v[2], rows)
     layer_out[...] = total.astype(BF16)
     arrived(rz.at[pl.ds(0, 2 * R - 1)], f_send)
-    arrived(far, far_send)
+
+
+def store_kernel(*refs):
+    sems = refs[8]
+    copies = [pltpu.make_async_copy(refs[n], refs[4 + n], sems.at[n]) for n in range(4)]
+    for copy in copies:
+        copy.start()
+    for copy in copies:
+        copy.wait()
 
 
 def body(tokens, grad_out, expert_ids, gate_scale, gate_weight, up_weight, down_weight):
@@ -475,7 +457,6 @@
             pltpu.VMEM((2 * R, C, Q), BF16),
             pltpu.VMEM((R, 2 * F, S), BF16),
             pltpu.VMEM((3, rows, R * S), BF16),
-            pltpu.VMEM((2, C // 2, Q), BF16),
             dma((7,)),
             dma((2, 3)),
             dma((R, 2, 3)),
@@ -487,8 +468,6 @@
             dma((2, R)),
             dma(()),
             dma(()),
-            dma(()),
-            dma((2,)),
         ],
         compiler_params=pltpu.CompilerParams(
             collective_id=0, has_side_effects=True, vmem_limit_bytes=48 * 1024 * 1024
@@ -507,6 +486,14 @@
             )
         )
     )
+    outs = pl.pallas_call(
+        store_kernel,
+        out_shape=tuple(jax.ShapeDtypeStruct(o.shape, o.dtype) for o in outs),
+        in_specs=[pl.BlockSpec(memory_space=pltpu.VMEM)] * 4,
+        out_specs=(hbm,) * 4,
+        scratch_shapes=[dma((4,))],
+        compiler_params=pltpu.CompilerParams(vmem_limit_bytes=8 * 1024 * 1024),
+    )(*outs)
     return (outs[0], outs[1][None], outs[2][None], outs[3][None])
 
 

time: 133 us -> 129 us (0.970); the launches traced: 132 us -> 126 us
  local copies, waits for them, and re-layouts: 3.29 us -> 0 us
  Pallas kernels: 128 us -> 126 us
    pallas_call x1, Pallas kernels: 128 us -> 124 us  [body(): pl.pallas_call(functools.partial(layer_kernel, nx, nz), out_shape=(jax.Sh...]
    unnamed x4 -> x0, local copies, waits for them, and re-layouts: 3.29 us -> none
    pallas_call x0 -> x1, Pallas kernels: none -> 1.48 us  [body(): pl.pallas_call(store_kernel, out_shape=tuple((jax.ShapeDtypeStruct(o.shap...]
where the time goes in v5:
time: 129 us; the launch traced here: 126 us
  Pallas kernels  126 us (98%)
    pallas_call x1, Pallas kernels, body(): pl.pallas_call(functools.partial(layer_kernel, nx, nz), out_shape=(jax.Sh...  124 us

profile of v5, /device:TPU:1, one launch (start us, length us, event | category | flops | bytes accessed | tf_op | source)
XLA Modules:
  0.0 126.5 jit_solution(10975952956160598341)
XLA Ops:
  0.6 124.4 %shard_map.102 = (bf16[128,512]{1,0:T(8,128)(2,1)S(1)}, bf16[192,2048]{1,0:T(8,128)(2,1)S(1)}, bf16[192,2048]{1,0:T(8,128)(2,1)S(1)}, bf16[768,512]{1,0:T(8,128)(2,1)S(1)}) custom-call(s32[4,128]{1,0:T(4,128)} %bitcast.11, f32[4,128]{1,0:T(4,128)} %bitcast.12, bf16[128,512]{1,0:T(8,128)(2,1)} %tok_hbm.1, bf16[128,512]{1,0:T(8,128)(2,1)} %grad_hbm.1, ...), custom_call_target="tpu_custom_call" | custom-call | tf_op jit(solution)/shard_map/pallas_call | solution.py:427
  125.0 1.5 %shard_map.103 = (bf16[128,512]{1,0:T(8,128)(2,1)}, bf16[192,2048]{1,0:T(8,128)(2,1)}, bf16[192,2048]{1,0:T(8,128)(2,1)}, bf16[768,512]{1,0:T(8,128)(2,1)}) custom-call(bf16[128,512]{1,0:T(8,128)(2,1)S(1)} %get-tuple-element.12.refs_0_, bf16[192,2048]{1,0:T(8,128)(2,1)S(1)} %get-tuple-element.13.refs_1_, bf16[192,2048]{1,0:T(8,128)(2,1)S(1)} %get-tuple-element.14.refs_2_, ...), custom_call_target="tpu_custom_call" | custom-call | tf_op jit(solution)/shard_map/pallas_call | solution.py:489

commit v6 on v5

--- a/solution.py
+++ b/solution.py
@@ -173,13 +173,13 @@
             src_ref=rz.at[2 * i + h],
             dst_ref=fin.at[2 * i + h],
             send_sem=f_send,
-            recv_sem=f_recv,
+            recv_sem=f_recv.at[i // (R - 2)],
             device_id=at_plane(z + i) if h == 0 else at_plane(z + nz - i - 1),
             device_id_type=MESH,
         )
 
     def return_own():
-        return pltpu.make_async_copy(rz.at[0], fin.at[0], f_recv)
+        return pltpu.make_async_copy(rz.at[0], fin.at[0], f_recv.at[0])
 
     def select(i):
         marks, weights = [], 0.0
@@ -398,9 +398,13 @@
     arrived(slot_t.at[pl.ds(0, 3)], y_send.at[0])
     arrived(hid.at[pl.ds(0, 3)], y_send.at[1])
     arrived(hgs, s_send)
-    arrived(fin, f_recv)
-    rows = fin[...].reshape(R * S, Q)
-    total = dot(place_v[0], rows) + dot(place_v[1], rows) + dot(place_v[2], rows)
+    near = 2 * (R - 2)
+    total = 0.0
+    for n, (low, count) in enumerate(((0, near), (near, 4))):
+        arrived(fin.at[pl.ds(low, count)], f_recv.at[n])
+        rows = fin[low : low + count].reshape(count * C, Q)
+        for part in range(3):
+            total = total + dot(place_v[part, :, low * C : (low + count) * C], rows)
     layer_out[...] = total.astype(BF16)
     arrived(rz.at[pl.ds(0, 2 * R - 1)], f_send)
 
@@ -467,7 +471,7 @@
             dma(()),
             dma((2, R)),
             dma(()),
-            dma(()),
+            dma((2,)),
         ],
         compiler_params=pltpu.CompilerParams(
             collective_id=0, has_side_effects=True, vmem_limit_bytes=48 * 1024 * 1024

time: 129 us -> 129 us (level)
  the two profiles are of different devices: /device:TPU:1 before, /device:TPU:69 now
where the time goes in v6:
time: 129 us
  Pallas kernels  128 us (99%)
    pallas_call x1, Pallas kernels, body(): pl.pallas_call(functools.partial(layer_kernel, nx, nz), out_shape=(jax.Sh...  126 us

profile of v6, /device:TPU:69, one launch (start us, length us, event | category | flops | bytes accessed | tf_op | source)
XLA Modules:
  0.0 128.6 jit_solution(16353488975363087388)
XLA Ops:
  0.6 126.5 %shard_map.102 = (bf16[128,512]{1,0:T(8,128)(2,1)S(1)}, bf16[192,2048]{1,0:T(8,128)(2,1)S(1)}, bf16[192,2048]{1,0:T(8,128)(2,1)S(1)}, bf16[768,512]{1,0:T(8,128)(2,1)S(1)}) custom-call(s32[4,128]{1,0:T(4,128)} %bitcast.11, f32[4,128]{1,0:T(4,128)} %bitcast.12, bf16[128,512]{1,0:T(8,128)(2,1)} %tok_hbm.1, bf16[128,512]{1,0:T(8,128)(2,1)} %grad_hbm.1, ...), custom_call_target="tpu_custom_call" | custom-call | tf_op jit(solution)/shard_map/pallas_call | solution.py:431
  127.1 1.5 %shard_map.103 = (bf16[128,512]{1,0:T(8,128)(2,1)}, bf16[192,2048]{1,0:T(8,128)(2,1)}, bf16[192,2048]{1,0:T(8,128)(2,1)}, bf16[768,512]{1,0:T(8,128)(2,1)}) custom-call(bf16[128,512]{1,0:T(8,128)(2,1)S(1)} %get-tuple-element.12.refs_0_, bf16[192,2048]{1,0:T(8,128)(2,1)S(1)} %get-tuple-element.13.refs_1_, bf16[192,2048]{1,0:T(8,128)(2,1)S(1)} %get-tuple-element.14.refs_2_, ...), custom_call_target="tpu_custom_call" | custom-call | tf_op jit(solution)/shard_map/pallas_call | solution.py:493
